TPU v7x, 512 devices: a whole 4x8x8 slice. The times are simulated.
512 devices in a mesh: branch: 8 (over z), cluster: 64 (over x, y, core).
Axes of the slice: x: 4, y: 8, z: 8, core: 2. Of those that a mesh axis runs over, the one named last changes fastest.
Arguments:
- charges: float32 [8192, 16, 256], P(('branch', 'cluster')), may hold values from -6 to 6
- coords: float32 [8192, 3, 256], P(('branch', 'cluster')), may hold values from -4 to 4
- areas: float32 [8192, 256], P(('branch', 'cluster')), may hold values from 0.1 to 1
- col_basis: float32 [8192, 64, 256], P(('branch', 'cluster')), may hold values from -0.375 to 0.375
- row_basis: float32 [8192, 64, 256], P(('branch', 'cluster')), may hold values from -0.75 to 0.75
- leaf_up: float32 [8192, 64, 64], P(('branch', 'cluster')), may hold values from -0.1875 to 0.1875
- leaf_down: float32 [8192, 64, 64], P(('branch', 'cluster')), may hold values from -0.75 to 0.75
- leaf_coupling: float32 [8192, 4, 64, 64], P(('branch', 'cluster')), may hold values from -0.375 to 0.375
- up_transfer: float32 [8, 6, 2, 64, 64], P('branch'), may hold values from -0.5 to 0.5
- down_transfer: float32 [8, 6, 2, 64, 64], P('branch'), may hold values from -0.75 to 0.75
- sibling_coupling: float32 [8, 6, 2, 64, 64], P('branch'), may hold values from -0.75 to 0.75
- branch_coupling: float32 [8, 7, 64, 64], P('branch'), may hold values from -0.25 to 0.25
- near_list: int32 [8192, 16], P(('branch', 'cluster')), may hold values from 0 to 8191, as said below
- far_list: int32 [8192, 4], P(('branch', 'cluster')), may hold values from 0 to 8191, as said below
Outputs:
- potential: float32 [8192, 16, 256], P(('branch', 'cluster'))
Inputs may be any that keep to these rules, and one draw needn't show every extreme that they name: `near_list`: row n names 16 distinct leaves of the same branch, each held by the device of leaf n or by one of its two neighbours along the cluster axis; the first entry is n itself. `far_list`: row n names 4 distinct leaves from the same window of three devices as near_list, none of them in row n of near_list.
All inputs are finite; a program needn't handle non-finite values.
Results may differ from a plain program's by a relative error of at most 0.00022.
Values sent between devices are 32-bit elements; how exact they have to be, the bound alone decides.
A program may use at most 64 MiB of HBM per device.

v0:
```python
import math

import jax
import jax.numpy as jnp
from jax import lax
from jax.sharding import PartitionSpec as P

highest = lax.Precision.HIGHEST
reg_square = 0.01
inv_four_pi = 0.25 / math.pi


def padded(block, sides, width):
    for axis, dim in sides:
        count = lax.axis_size(axis)
        forward = [(i, i + 1) for i in range(count - 1)]
        backward = [(target, source) for source, target in forward]
        low = lax.ppermute(
            lax.slice_in_dim(block, block.shape[dim] - width, None, axis=dim), axis, forward
        )
        high = lax.ppermute(lax.slice_in_dim(block, 0, width, axis=dim), axis, backward)
        block = jnp.concatenate([low, block, high], axis=dim)
    return block


def from_partner(shard, axis, apart):
    return lax.ppermute(shard, axis, [(i, i ^ 1 << apart) for i in range(lax.axis_size(axis))])


def on_device(
    charges,
    coords,
    areas,
    col_basis,
    row_basis,
    leaf_up,
    leaf_down,
    leaf_coupling,
    up_transfer,
    down_transfer,
    sibling_coupling,
    branch_coupling,
    near_list,
    far_list,
):
    leaves, scenarios, panels = charges.shape
    clusters = lax.axis_size("cluster")
    levels = clusters.bit_length() - 1
    cluster_idx = lax.axis_index("cluster")
    branch_idx = lax.axis_index("branch")
    first_leaf = (branch_idx * clusters + cluster_idx) * leaves
    leaf_coef = jnp.einsum("lkp,lsp->lks", col_basis, charges, precision=highest)
    leaf_pack = jnp.concatenate([charges, coords, areas[:, None, :]], axis=1)
    source_pack = padded(leaf_pack, (("cluster", 0),), leaves)
    coef_extended = padded(leaf_coef, (("cluster", 0),), leaves)
    near_local = near_list - first_leaf + leaves

    def add_slot(slot_index, running):
        column_ids = lax.dynamic_slice_in_dim(near_local, slot_index, 1, 1)[:, 0]
        source = jnp.take(source_pack, column_ids, axis=0)
        src_charge = source[:, :scenarios]
        src_area = source[:, scenarios + 3]
        dist_square = jnp.zeros((leaves, panels, panels), jnp.float32)
        for axis_index in range(3):
            offset = coords[:, axis_index, :, None] - source[:, scenarios + axis_index, None, :]
            dist_square = dist_square + offset * offset
        kernel = src_area[:, None, :] * inv_four_pi / jnp.sqrt(dist_square + reg_square)
        return running + jnp.einsum("lpq,lsq->lsp", kernel, src_charge, precision=highest)

    near_part = lax.fori_loop(
        0, near_list.shape[1], add_slot, jnp.zeros((leaves, scenarios, panels), jnp.float32)
    )
    far_local = far_list - first_leaf + leaves
    far_coef = jnp.take(coef_extended, far_local, axis=0)
    leaf_local = jnp.einsum("ljac,ljcs->las", leaf_coupling, far_coef, precision=highest)
    node_coef = jnp.einsum("lac,lcs->as", leaf_up, leaf_coef, precision=highest)
    up_mats = up_transfer[0]
    siblings = []
    current = node_coef
    for level_index in range(levels):
        sibling = from_partner(current, "cluster", level_index)
        parity = cluster_idx >> level_index & 1
        left_child = jnp.where(parity == 0, current, sibling)
        right_child = jnp.where(parity == 0, sibling, current)
        current = jnp.dot(up_mats[level_index, 0], left_child, precision=highest) + jnp.dot(
            up_mats[level_index, 1], right_child, precision=highest
        )
        siblings.append(sibling)
    branch_roots = lax.all_gather(current[None], "branch", axis=0, tiled=True)
    branch_count = branch_roots.shape[0]
    partner_ids = (branch_idx + 1 + jnp.arange(branch_count - 1)) % branch_count
    partner_roots = jnp.take(branch_roots, partner_ids, axis=0)
    downward = jnp.einsum("iac,ics->as", branch_coupling[0], partner_roots, precision=highest)
    for level_index in reversed(range(levels)):
        parity = cluster_idx >> level_index & 1
        sib_mat = jnp.take(sibling_coupling[0, level_index], parity, axis=0)
        down_mat = jnp.take(down_transfer[0, level_index], parity, axis=0)
        downward = jnp.dot(sib_mat, siblings[level_index], precision=highest) + jnp.dot(
            down_mat, downward, precision=highest
        )
    leaf_total = leaf_local + jnp.einsum("lac,cs->las", leaf_down, downward, precision=highest)
    return jnp.einsum("lkp,lks->lsp", row_basis, leaf_total, precision=highest) + near_part


def solution(mesh):
    in_specs = (
        P(("branch", "cluster"), None, None),
        P(("branch", "cluster"), None, None),
        P(("branch", "cluster"), None),
        P(("branch", "cluster"), None, None),
        P(("branch", "cluster"), None, None),
        P(("branch", "cluster"), None, None),
        P(("branch", "cluster"), None, None),
        P(("branch", "cluster"), None, None, None),
        P("branch", None, None, None, None),
        P("branch", None, None, None, None),
        P("branch", None, None, None, None),
        P("branch", None, None, None),
        P(("branch", "cluster"), None),
        P(("branch", "cluster"), None),
    )
    out_specs = P(("branch", "cluster"), None, None)
    return jax.shard_map(
        on_device, mesh=mesh, in_specs=in_specs, out_specs=out_specs, check_vma=False
    )
```

profile of v0, /device:TPU:4, one launch (start us, length us, event | category | flops | bytes accessed | tf_op | source)
XLA Modules:
  0.0 265.2 jit_solution(13807745674813303443)
XLA Ops:
  4.4 5.8 %collective-permute-start.1 = (f32[16,64,16]{1,2,0:T(8,128)S(1)}, f32[16,64,16]{1,2,0:T(8,128)}, u32[]{:S(2)}, u32[]{:S(2)}) collective-permute-start(f32[16,64,16]{1,2,0:T(8,128)S(1)} %fusion.165), channel_id=1, source_target_pairs={{1,0},{2,1},{3,2},{4,3},{5,4},{6,5},{7,6},{8,7},{9,8},{10,9},{11,1... | collective-permute-start | bytes 196616 | tf_op jit(solution)/shard_map/ppermute | solution.py:21
  15.4 5.8 %collective-permute-start.9 = (f32[16,20,256]{2,1,0:T(8,128)}, f32[16,20,256]{2,1,0:T(8,128)}, u32[]{:S(2)}, u32[]{:S(2)}) collective-permute-start(f32[16,20,256]{2,1,0:T(8,128)} %pad_maximum_fusion.2), channel_id=1, source_target_pairs={{1,0},{2,1},{3,2},{4,3},{5,4},{6,5},{7,6},{8,7},{9,8},{10,9},{11,1... | collective-permute-start | bytes 983048 | tf_op jit(solution)/shard_map/ppermute | solution.py:21
  36.3 4.2 %collective-permute-done.4 = f32[64,16]{0,1:T(8,128)S(1)} collective-permute-done((f32[64,16]{0,1:T(8,128)S(1)}, f32[64,16]{0,1:T(8,128)S(1)}, u32[]{:S(2)}, u32[]{:S(2)}) %collective-permute-start.4) | collective-permute-done | bytes 4128 | tf_op jit(solution)/shard_map/ppermute | solution.py:27
  40.9 6.0 %collective-permute-start.5 = (f32[64,16]{0,1:T(8,128)S(1)}, f32[64,16]{0,1:T(8,128)S(1)}, u32[]{:S(2)}, u32[]{:S(2)}) collective-permute-start(f32[64,16]{0,1:T(8,128)S(1)} %fusion.29), channel_id=1, source_target_pairs={{0,8},{1,9},{2,10},{3,11},{4,12},{5,13},{6,14},{7,15},{8,0},{9,1},... | collective-permute-start | bytes 12296 | tf_op jit(solution)/shard_map/ppermute | solution.py:27
  47.0 3.3 %collective-permute-done.5 = f32[64,16]{0,1:T(8,128)S(1)} collective-permute-done((f32[64,16]{0,1:T(8,128)S(1)}, f32[64,16]{0,1:T(8,128)S(1)}, u32[]{:S(2)}, u32[]{:S(2)}) %collective-permute-start.5) | collective-permute-done | bytes 4128 | tf_op jit(solution)/shard_map/ppermute | solution.py:27
  58.6 5.0 %collective-permute-done.7 = f32[64,16]{0,1:T(8,128)S(1)} collective-permute-done((f32[64,16]{0,1:T(8,128)S(1)}, f32[64,16]{0,1:T(8,128)S(1)}, u32[]{:S(2)}, u32[]{:S(2)}) %collective-permute-start.7) | collective-permute-done | bytes 4128 | tf_op jit(solution)/shard_map/ppermute | solution.py:27
  63.9 31.0 %all-gather.1 = f32[8,64,16]{1,2,0:T(8,128)S(1)} all-gather(f32[1,64,16]{1,2,0:T(8,128)S(1)} %fusion.26), channel_id=2, replica_groups=mesh['branch'=8,'cluster'=64] {'branch'}, dimensions={0}, use_global_device_ids=true | all-gather | bytes 36864 | tf_op jit(solution)/shard_map/all_gather | solution.py:89
  111.1 152.4 %while.15 = (s32[]{:T(128)}, f32[16,16,256]{2,1,0:T(8,128)}, s32[16,16]{0,1:T(8,128)S(1)}, f32[48,20,256]{2,1,0:T(8,128)}, f32[16,3,256]{2,0,1:T(8,128)S(1)}, /*index=5*/s32[]{:T(128)}, s32[]{:T(128)}) while((s32[]{:T(128)}, f32[16,16,256]{2,1,0:T(8,128)}, s32[16,16]{0,1:T(8,128)S(1)}, f32[48,20,256]{2,1,0:T(8,128)}, ...), condition=%wide.region_1.3_spmd.clone, body=%wide.region_0.2_spmd.clone.sunk | while | flops 212030560 | bytes 2585011 | solution.py:70
  113.7 6.1 %fusion.193 = f32[16,16,256]{2,1,0:T(8,128)} fusion(f32[16,256]{1,0:T(8,128)S(1)} %get-tuple-element.215, f32[16,256]{1,0:T(8,128)S(1)} %get-tuple-element.216, f32[16,256]{1,0:T(8,128)S(1)} %get-tuple-element.217, f32[16,256]{1,0:T(8,128)S(1)} %get-tuple-element.218, f32[16,256]{1,0:T(8,128)S(1)} %get-tuple-element.221, ...), kind=kOutput, calls=%fused_computation.23.clone.1 | convolution fusion | flops 211943424 | bytes 901121 | tf_op jit(solution)/shard_map/while/body/eval_jaxpr/lpq,lsq->lsp/dot_general | solution.py:68
  122.5 6.9 %fusion.193 = f32[16,16,256]{2,1,0:T(8,128)} fusion(f32[16,256]{1,0:T(8,128)S(1)} %get-tuple-element.215, f32[16,256]{1,0:T(8,128)S(1)} %get-tuple-element.216, f32[16,256]{1,0:T(8,128)S(1)} %get-tuple-element.217, f32[16,256]{1,0:T(8,128)S(1)} %get-tuple-element.218, f32[16,256]{1,0:T(8,128)S(1)} %get-tuple-element.221, ...), kind=kOutput, calls=%fused_computation.23.clone.1 | convolution fusion | flops 211943424 | bytes 901121 | tf_op jit(solution)/shard_map/while/body/eval_jaxpr/lpq,lsq->lsp/dot_general | solution.py:68
  132.1 6.9 %fusion.193 = f32[16,16,256]{2,1,0:T(8,128)} fusion(f32[16,256]{1,0:T(8,128)S(1)} %get-tuple-element.215, f32[16,256]{1,0:T(8,128)S(1)} %get-tuple-element.216, f32[16,256]{1,0:T(8,128)S(1)} %get-tuple-element.217, f32[16,256]{1,0:T(8,128)S(1)} %get-tuple-element.218, f32[16,256]{1,0:T(8,128)S(1)} %get-tuple-element.221, ...), kind=kOutput, calls=%fused_computation.23.clone.1 | convolution fusion | flops 211943424 | bytes 901121 | tf_op jit(solution)/shard_map/while/body/eval_jaxpr/lpq,lsq->lsp/dot_general | solution.py:68
  141.6 6.9 %fusion.193 = f32[16,16,256]{2,1,0:T(8,128)} fusion(f32[16,256]{1,0:T(8,128)S(1)} %get-tuple-element.215, f32[16,256]{1,0:T(8,128)S(1)} %get-tuple-element.216, f32[16,256]{1,0:T(8,128)S(1)} %get-tuple-element.217, f32[16,256]{1,0:T(8,128)S(1)} %get-tuple-element.218, f32[16,256]{1,0:T(8,128)S(1)} %get-tuple-element.221, ...), kind=kOutput, calls=%fused_computation.23.clone.1 | convolution fusion | flops 211943424 | bytes 901121 | tf_op jit(solution)/shard_map/while/body/eval_jaxpr/lpq,lsq->lsp/dot_general | solution.py:68
  151.2 6.9 %fusion.193 = f32[16,16,256]{2,1,0:T(8,128)} fusion(f32[16,256]{1,0:T(8,128)S(1)} %get-tuple-element.215, f32[16,256]{1,0:T(8,128)S(1)} %get-tuple-element.216, f32[16,256]{1,0:T(8,128)S(1)} %get-tuple-element.217, f32[16,256]{1,0:T(8,128)S(1)} %get-tuple-element.218, f32[16,256]{1,0:T(8,128)S(1)} %get-tuple-element.221, ...), kind=kOutput, calls=%fused_computation.23.clone.1 | convolution fusion | flops 211943424 | bytes 901121 | tf_op jit(solution)/shard_map/while/body/eval_jaxpr/lpq,lsq->lsp/dot_general | solution.py:68
  160.8 6.9 %fusion.193 = f32[16,16,256]{2,1,0:T(8,128)} fusion(f32[16,256]{1,0:T(8,128)S(1)} %get-tuple-element.215, f32[16,256]{1,0:T(8,128)S(1)} %get-tuple-element.216, f32[16,256]{1,0:T(8,128)S(1)} %get-tuple-element.217, f32[16,256]{1,0:T(8,128)S(1)} %get-tuple-element.218, f32[16,256]{1,0:T(8,128)S(1)} %get-tuple-element.221, ...), kind=kOutput, calls=%fused_computation.23.clone.1 | convolution fusion | flops 211943424 | bytes 901121 | tf_op jit(solution)/shard_map/while/body/eval_jaxpr/lpq,lsq->lsp/dot_general | solution.py:68
  170.4 6.9 %fusion.193 = f32[16,16,256]{2,1,0:T(8,128)} fusion(f32[16,256]{1,0:T(8,128)S(1)} %get-tuple-element.215, f32[16,256]{1,0:T(8,128)S(1)} %get-tuple-element.216, f32[16,256]{1,0:T(8,128)S(1)} %get-tuple-element.217, f32[16,256]{1,0:T(8,128)S(1)} %get-tuple-element.218, f32[16,256]{1,0:T(8,128)S(1)} %get-tuple-element.221, ...), kind=kOutput, calls=%fused_computation.23.clone.1 | convolution fusion | flops 211943424 | bytes 901121 | tf_op jit(solution)/shard_map/while/body/eval_jaxpr/lpq,lsq->lsp/dot_general | solution.py:68
  179.9 6.9 %fusion.193 = f32[16,16,256]{2,1,0:T(8,128)} fusion(f32[16,256]{1,0:T(8,128)S(1)} %get-tuple-element.215, f32[16,256]{1,0:T(8,128)S(1)} %get-tuple-element.216, f32[16,256]{1,0:T(8,128)S(1)} %get-tuple-element.217, f32[16,256]{1,0:T(8,128)S(1)} %get-tuple-element.218, f32[16,256]{1,0:T(8,128)S(1)} %get-tuple-element.221, ...), kind=kOutput, calls=%fused_computation.23.clone.1 | convolution fusion | flops 211943424 | bytes 901121 | tf_op jit(solution)/shard_map/while/body/eval_jaxpr/lpq,lsq->lsp/dot_general | solution.py:68
  189.5 6.9 %fusion.193 = f32[16,16,256]{2,1,0:T(8,128)} fusion(f32[16,256]{1,0:T(8,128)S(1)} %get-tuple-element.215, f32[16,256]{1,0:T(8,128)S(1)} %get-tuple-element.216, f32[16,256]{1,0:T(8,128)S(1)} %get-tuple-element.217, f32[16,256]{1,0:T(8,128)S(1)} %get-tuple-element.218, f32[16,256]{1,0:T(8,128)S(1)} %get-tuple-element.221, ...), kind=kOutput, calls=%fused_computation.23.clone.1 | convolution fusion | flops 211943424 | bytes 901121 | tf_op jit(solution)/shard_map/while/body/eval_jaxpr/lpq,lsq->lsp/dot_general | solution.py:68
  199.1 6.9 %fusion.193 = f32[16,16,256]{2,1,0:T(8,128)} fusion(f32[16,256]{1,0:T(8,128)S(1)} %get-tuple-element.215, f32[16,256]{1,0:T(8,128)S(1)} %get-tuple-element.216, f32[16,256]{1,0:T(8,128)S(1)} %get-tuple-element.217, f32[16,256]{1,0:T(8,128)S(1)} %get-tuple-element.218, f32[16,256]{1,0:T(8,128)S(1)} %get-tuple-element.221, ...), kind=kOutput, calls=%fused_computation.23.clone.1 | convolution fusion | flops 211943424 | bytes 901121 | tf_op jit(solution)/shard_map/while/body/eval_jaxpr/lpq,lsq->lsp/dot_general | solution.py:68
  208.7 6.9 %fusion.193 = f32[16,16,256]{2,1,0:T(8,128)} fusion(f32[16,256]{1,0:T(8,128)S(1)} %get-tuple-element.215, f32[16,256]{1,0:T(8,128)S(1)} %get-tuple-element.216, f32[16,256]{1,0:T(8,128)S(1)} %get-tuple-element.217, f32[16,256]{1,0:T(8,128)S(1)} %get-tuple-element.218, f32[16,256]{1,0:T(8,128)S(1)} %get-tuple-element.221, ...), kind=kOutput, calls=%fused_computation.23.clone.1 | convolution fusion | flops 211943424 | bytes 901121 | tf_op jit(solution)/shard_map/while/body/eval_jaxpr/lpq,lsq->lsp/dot_general | solution.py:68
  218.2 6.9 %fusion.193 = f32[16,16,256]{2,1,0:T(8,128)} fusion(f32[16,256]{1,0:T(8,128)S(1)} %get-tuple-element.215, f32[16,256]{1,0:T(8,128)S(1)} %get-tuple-element.216, f32[16,256]{1,0:T(8,128)S(1)} %get-tuple-element.217, f32[16,256]{1,0:T(8,128)S(1)} %get-tuple-element.218, f32[16,256]{1,0:T(8,128)S(1)} %get-tuple-element.221, ...), kind=kOutput, calls=%fused_computation.23.clone.1 | convolution fusion | flops 211943424 | bytes 901121 | tf_op jit(solution)/shard_map/while/body/eval_jaxpr/lpq,lsq->lsp/dot_general | solution.py:68
  227.8 6.9 %fusion.193 = f32[16,16,256]{2,1,0:T(8,128)} fusion(f32[16,256]{1,0:T(8,128)S(1)} %get-tuple-element.215, f32[16,256]{1,0:T(8,128)S(1)} %get-tuple-element.216, f32[16,256]{1,0:T(8,128)S(1)} %get-tuple-element.217, f32[16,256]{1,0:T(8,128)S(1)} %get-tuple-element.218, f32[16,256]{1,0:T(8,128)S(1)} %get-tuple-element.221, ...), kind=kOutput, calls=%fused_computation.23.clone.1 | convolution fusion | flops 211943424 | bytes 901121 | tf_op jit(solution)/shard_map/while/body/eval_jaxpr/lpq,lsq->lsp/dot_general | solution.py:68
  237.4 6.9 %fusion.193 = f32[16,16,256]{2,1,0:T(8,128)} fusion(f32[16,256]{1,0:T(8,128)S(1)} %get-tuple-element.215, f32[16,256]{1,0:T(8,128)S(1)} %get-tuple-element.216, f32[16,256]{1,0:T(8,128)S(1)} %get-tuple-element.217, f32[16,256]{1,0:T(8,128)S(1)} %get-tuple-element.218, f32[16,256]{1,0:T(8,128)S(1)} %get-tuple-element.221, ...), kind=kOutput, calls=%fused_computation.23.clone.1 | convolution fusion | flops 211943424 | bytes 901121 | tf_op jit(solution)/shard_map/while/body/eval_jaxpr/lpq,lsq->lsp/dot_general | solution.py:68
  247.0 6.9 %fusion.193 = f32[16,16,256]{2,1,0:T(8,128)} fusion(f32[16,256]{1,0:T(8,128)S(1)} %get-tuple-element.215, f32[16,256]{1,0:T(8,128)S(1)} %get-tuple-element.216, f32[16,256]{1,0:T(8,128)S(1)} %get-tuple-element.217, f32[16,256]{1,0:T(8,128)S(1)} %get-tuple-element.218, f32[16,256]{1,0:T(8,128)S(1)} %get-tuple-element.221, ...), kind=kOutput, calls=%fused_computation.23.clone.1 | convolution fusion | flops 211943424 | bytes 901121 | tf_op jit(solution)/shard_map/while/body/eval_jaxpr/lpq,lsq->lsp/dot_general | solution.py:68
  256.5 6.9 %fusion.193 = f32[16,16,256]{2,1,0:T(8,128)} fusion(f32[16,256]{1,0:T(8,128)S(1)} %get-tuple-element.215, f32[16,256]{1,0:T(8,128)S(1)} %get-tuple-element.216, f32[16,256]{1,0:T(8,128)S(1)} %get-tuple-element.217, f32[16,256]{1,0:T(8,128)S(1)} %get-tuple-element.218, f32[16,256]{1,0:T(8,128)S(1)} %get-tuple-element.221, ...), kind=kOutput, calls=%fused_computation.23.clone.1 | convolution fusion | flops 211943424 | bytes 901121 | tf_op jit(solution)/shard_map/while/body/eval_jaxpr/lpq,lsq->lsp/dot_general | solution.py:68
  (283 shorter events, 92.8 us)
Async XLA Ops:
  0.0 104.9 %copy-start = (f32[16,4,64,64]{3,2,1,0:T(8,128)S(1)}, f32[16,4,64,64]{3,2,1,0:T(8,128)}, u32[]{:S(2)}) copy-start(f32[16,4,64,64]{3,2,1,0:T(8,128)} %param.25) | copy-start | bytes 3145732
  0.0 21.1 %copy-start.5 = (f32[16,64,64]{2,1,0:T(8,128)S(1)}, f32[16,64,64]{2,1,0:T(8,128)}, u32[]{:S(2)}) copy-start(f32[16,64,64]{2,1,0:T(8,128)} %param.23) | copy-start | bytes 786436
  0.0 24.2 %copy-start.6 = (f32[1,6,2,64,64]{4,3,2,1,0:T(8,128)S(1)}, f32[1,6,2,64,64]{4,3,2,1,0:T(8,128)}, u32[]{:S(2)}) copy-start(f32[1,6,2,64,64]{4,3,2,1,0:T(8,128)} %param.27) | copy-start | bytes 589828
  0.0 24.9 %copy-start.7 = (f32[1,6,2,64,64]{4,3,2,1,0:T(8,128)S(1)}, f32[1,6,2,64,64]{4,3,2,1,0:T(8,128)}, u32[]{:S(2)}) copy-start(f32[1,6,2,64,64]{4,3,2,1,0:T(8,128)} %param.28) | copy-start | bytes 589828
  0.0 26.4 %copy-start.8 = (f32[1,6,2,64,64]{4,3,2,1,0:T(8,128)S(1)}, f32[1,6,2,64,64]{4,3,2,1,0:T(8,128)}, u32[]{:S(2)}) copy-start(f32[1,6,2,64,64]{4,3,2,1,0:T(8,128)} %param.26) | copy-start | bytes 589828
  2.4 100.8 %collective-permute-start = (f32[16,64,16]{1,2,0:T(8,128)S(1)}, f32[16,64,16]{1,2,0:T(8,128)}, u32[]{:S(2)}, u32[]{:S(2)}) collective-permute-start(f32[16,64,16]{1,2,0:T(8,128)S(1)} %fusion.165), channel_id=1, source_target_pairs={{0,1},{1,2},{2,3},{3,4},{4,5},{5,6},{6,7},{7,8},{8,9},{9,10},{10,1... | collective-permute-start | bytes 196616 | tf_op jit(solution)/shard_map/ppermute | solution.py:18
  4.4 98.9 %collective-permute-start.1 = (f32[16,64,16]{1,2,0:T(8,128)S(1)}, f32[16,64,16]{1,2,0:T(8,128)}, u32[]{:S(2)}, u32[]{:S(2)}) collective-permute-start(f32[16,64,16]{1,2,0:T(8,128)S(1)} %fusion.165), channel_id=1, source_target_pairs={{1,0},{2,1},{3,2},{4,3},{5,4},{6,5},{7,6},{8,7},{9,8},{10,9},{11,1... | collective-permute-start | bytes 196616 | tf_op jit(solution)/shard_map/ppermute | solution.py:21
  13.4 95.3 %collective-permute-start.8 = (f32[16,20,256]{2,1,0:T(8,128)}, f32[16,20,256]{2,1,0:T(8,128)}, u32[]{:S(2)}, u32[]{:S(2)}) collective-permute-start(f32[16,20,256]{2,1,0:T(8,128)} %pad_maximum_fusion.2), channel_id=1, source_target_pairs={{0,1},{1,2},{2,3},{3,4},{4,5},{5,6},{6,7},{7,8},{8,9},{9,10},{10,1... | collective-permute-start | bytes 983048 | tf_op jit(solution)/shard_map/ppermute | solution.py:18
  15.4 93.4 %collective-permute-start.9 = (f32[16,20,256]{2,1,0:T(8,128)}, f32[16,20,256]{2,1,0:T(8,128)}, u32[]{:S(2)}, u32[]{:S(2)}) collective-permute-start(f32[16,20,256]{2,1,0:T(8,128)} %pad_maximum_fusion.2), channel_id=1, source_target_pairs={{1,0},{2,1},{3,2},{4,3},{5,4},{6,5},{7,6},{8,7},{9,8},{10,9},{11,1... | collective-permute-start | bytes 983048 | tf_op jit(solution)/shard_map/ppermute | solution.py:21
  22.3 4.2 %collective-permute-start.2 = (f32[64,16]{0,1:T(8,128)}, f32[64,16]{0,1:T(8,128)}, u32[]{:S(2)}, u32[]{:S(2)}) collective-permute-start(f32[64,16]{0,1:T(8,128)} %convolution_bitcast_fusion.3), channel_id=1, source_target_pairs={{0,1},{1,0},{2,3},{3,2},{4,5},{5,4},{6,7},{7,6},{8,9},{9,8},{10,11... | collective-permute-start | bytes 12296 | tf_op jit(solution)/shard_map/ppermute | solution.py:27
  25.0 70.5 %copy-start.9 = (f32[1,7,64,64]{3,2,1,0:T(8,128)S(1)}, f32[1,7,64,64]{3,2,1,0:T(8,128)}, u32[]{:S(2)}) copy-start(f32[1,7,64,64]{3,2,1,0:T(8,128)} %param.29) | copy-start | bytes 344068
  25.6 75.8 %copy-start.12 = (f32[2,64,64]{2,1,0:T(8,128)S(1)}, f32[2,64,64]{2,1,0:T(8,128)}, u32[]{:S(2)}) copy-start(f32[2,64,64]{2,1,0:T(8,128)} %get-tuple-element.163) | copy-start | bytes 98308
  25.6 76.2 %copy-start.11 = (f32[2,64,64]{2,1,0:T(8,128)S(1)}, f32[2,64,64]{2,1,0:T(8,128)}, u32[]{:S(2)}) copy-start(f32[2,64,64]{2,1,0:T(8,128)} %get-tuple-element.164) | copy-start | bytes 98308
  25.7 76.5 %copy-start.10 = (f32[2,64,64]{2,1,0:T(8,128)S(1)}, f32[2,64,64]{2,1,0:T(8,128)}, u32[]{:S(2)}) copy-start(f32[2,64,64]{2,1,0:T(8,128)} %get-tuple-element.161) | copy-start | bytes 98308
  28.2 5.6 %collective-permute-start.3 = (f32[64,16]{0,1:T(8,128)S(1)}, f32[64,16]{0,1:T(8,128)S(1)}, u32[]{:S(2)}, u32[]{:S(2)}) collective-permute-start(f32[64,16]{0,1:T(8,128)S(1)} %fusion.31), channel_id=1, source_target_pairs={{0,2},{1,3},{2,0},{3,1},{4,6},{5,7},{6,4},{7,5},{8,10},{9,11},{10,... | collective-permute-start | bytes 12296 | tf_op jit(solution)/shard_map/ppermute | solution.py:27
  34.1 6.5 %collective-permute-start.4 = (f32[64,16]{0,1:T(8,128)S(1)}, f32[64,16]{0,1:T(8,128)S(1)}, u32[]{:S(2)}, u32[]{:S(2)}) collective-permute-start(f32[64,16]{0,1:T(8,128)S(1)} %fusion.30), channel_id=1, source_target_pairs={{0,4},{1,5},{2,6},{3,7},{4,0},{5,1},{6,2},{7,3},{8,12},{9,13},{10,... | collective-permute-start | bytes 12296 | tf_op jit(solution)/shard_map/ppermute | solution.py:27
  40.9 9.5 %collective-permute-start.5 = (f32[64,16]{0,1:T(8,128)S(1)}, f32[64,16]{0,1:T(8,128)S(1)}, u32[]{:S(2)}, u32[]{:S(2)}) collective-permute-start(f32[64,16]{0,1:T(8,128)S(1)} %fusion.29), channel_id=1, source_target_pairs={{0,8},{1,9},{2,10},{3,11},{4,12},{5,13},{6,14},{7,15},{8,0},{9,1},... | collective-permute-start | bytes 12296 | tf_op jit(solution)/shard_map/ppermute | solution.py:27
  50.7 5.6 %collective-permute-start.6 = (f32[64,16]{0,1:T(8,128)S(1)}, f32[64,16]{0,1:T(8,128)S(1)}, u32[]{:S(2)}, u32[]{:S(2)}) collective-permute-start(f32[64,16]{0,1:T(8,128)S(1)} %fusion.28), channel_id=1, source_target_pairs={{0,16},{1,17},{2,18},{3,19},{4,20},{5,21},{6,22},{7,23},{8,24},{9,... | collective-permute-start | bytes 12296 | tf_op jit(solution)/shard_map/ppermute | solution.py:27
  56.5 7.1 %collective-permute-start.7 = (f32[64,16]{0,1:T(8,128)S(1)}, f32[64,16]{0,1:T(8,128)S(1)}, u32[]{:S(2)}, u32[]{:S(2)}) collective-permute-start(f32[64,16]{0,1:T(8,128)S(1)} %fusion.27), channel_id=1, source_target_pairs={{0,32},{1,33},{2,34},{3,35},{4,36},{5,37},{6,38},{7,39},{8,40},{9,... | collective-permute-start | bytes 12296 | tf_op jit(solution)/shard_map/ppermute | solution.py:27
  141.6 6.9 %copy-start.14 = (s32[16,16]{0,1:T(8,128)S(1)}, s32[16,16]{0,1:T(8,128)}, u32[]{:S(2)}) copy-start(s32[16,16]{0,1:T(8,128)} %copy-done.13) | copy-start | bytes 3076 | tf_op jit(solution)/shard_map/while
  151.2 6.9 %copy-start.14 = (s32[16,16]{0,1:T(8,128)S(1)}, s32[16,16]{0,1:T(8,128)}, u32[]{:S(2)}) copy-start(s32[16,16]{0,1:T(8,128)} %copy-done.13) | copy-start | bytes 3076 | tf_op jit(solution)/shard_map/while
  160.8 6.9 %copy-start.14 = (s32[16,16]{0,1:T(8,128)S(1)}, s32[16,16]{0,1:T(8,128)}, u32[]{:S(2)}) copy-start(s32[16,16]{0,1:T(8,128)} %copy-done.13) | copy-start | bytes 3076 | tf_op jit(solution)/shard_map/while
  170.4 6.9 %copy-start.14 = (s32[16,16]{0,1:T(8,128)S(1)}, s32[16,16]{0,1:T(8,128)}, u32[]{:S(2)}) copy-start(s32[16,16]{0,1:T(8,128)} %copy-done.13) | copy-start | bytes 3076 | tf_op jit(solution)/shard_map/while
  179.9 6.9 %copy-start.14 = (s32[16,16]{0,1:T(8,128)S(1)}, s32[16,16]{0,1:T(8,128)}, u32[]{:S(2)}) copy-start(s32[16,16]{0,1:T(8,128)} %copy-done.13) | copy-start | bytes 3076 | tf_op jit(solution)/shard_map/while
  (31 other events, 98.1 us)
where the time goes:
time: 268 us; the launch traced here: 265 us
  matrix products  128 us (48%)
  local copies, waits for them, and re-layouts  44.2 us (16%)
  starting transfers between devices  32.4 us (12%)
  blocking collectives  31 us (12%)
  waiting for transfers between devices  17.8 us (7%)
  other arithmetic  10 us (4%)
    dot_general x16, matrix products, add_slot(): jnp.einsum('lpq,lsq->lsp', kernel, src_charge, precision=highest)  110 us
    all_gather x1, blocking collectives, on_device(): branch_roots = lax.all_gather(current[None], 'branch', axis=0, tiled=True)  31 us
    gather x16, local copies, waits for them, and re-layouts, add_slot(): source = jnp.take(source_pack, column_ids, axis=0)  29.4 us
    ppermute x6, waiting for transfers between devices, from_partner(): lax.ppermute(shard, axis, [(i, i ^ 1 << apart) for i in range(lax.axis_si...  17.8 us
    ppermute x6, starting transfers between devices, from_partner(): lax.ppermute(shard, axis, [(i, i ^ 1 << apart) for i in range(lax.axis_si...  17.1 us
    ppermute x2, starting transfers between devices, padded(): lax.ppermute(lax.slice_in_dim(block, 0, width, axis=dim), axis, backward)  11.5 us
    while x96, local copies, waits for them, and re-layouts  9.26 us
  transfers between devices with their start and end apart: 10, of which 5 were waited for; matrix products, arithmetic and copies ran while one was open for 9% of the time, Pallas kernels for 0%

commit v1 on v0

v1 whole, which is shorter than its diff:
```python
import functools
import math

import jax
import jax.numpy as jnp
from jax import lax
from jax.experimental import pallas as pl
from jax.experimental.pallas import tpu as pltpu
from jax.sharding import PartitionSpec as P

f32, bf16 = jnp.float32, jnp.bfloat16
MESH = pl.DeviceIdType.MESH
reg_square = 0.01
inv_four_pi = 0.25 / math.pi

LEAVES, SCEN, PANELS, RANK = 16, 16, 256, 64
NEAR, FAR, LEVELS = 16, 4, 6
NX, NY, NZ, CLUSTERS = 4, 8, 8, 64
FEATURES = 32
PAIRS = ((0, 0), (0, 1), (1, 0), (0, 2), (2, 0), (1, 1), (1, 2), (2, 1))


def dot(a, b, ca, cb):
    return lax.dot_general(a, b, (((ca,), (cb,)), ((), ())), preferred_element_type=f32)


def halves(x):
    high = x.astype(bf16)
    return high, (x - high.astype(f32)).astype(bf16)


def dot3(a, b, cb=1):
    ah, al = halves(a)
    bh, bl = halves(b)
    return dot(ah, bh, 1, cb) + dot(al, bh, 1, cb) + dot(ah, bl, 1, cb)


def features(point, is_source):
    row = lax.broadcasted_iota(jnp.int32, (FEATURES, PANELS), 0)
    dim = row % 3
    coord_row = row < 24
    x, y, z = (jnp.broadcast_to(point[i : i + 1], (FEATURES, PANELS)) for i in range(3))
    square = x * x + y * y + z * z
    value = jnp.where(dim == 0, x, jnp.where(dim == 1, y, z))
    pair = row // 3
    part = jnp.zeros_like(row)
    side = 0 if is_source else 1
    for index, parts in enumerate(PAIRS):
        if parts[side]:
            part = jnp.where(pair == index, parts[side], part)
    if is_source:
        value = jnp.where(coord_row, value, jnp.where(pair == 8, square, 1.0))
        part = jnp.where(pair == 8, dim, part)
    else:
        value = jnp.where(coord_row, -2.0 * value, jnp.where(pair == 8, 1.0, square + reg_square))
        part = jnp.where(pair == 9, dim, part)
    value = jnp.where(row < 30, value, 0.0)
    high = value.astype(bf16).astype(f32)
    rest = value - high
    middle = rest.astype(bf16).astype(f32)
    low = rest - middle
    return jnp.where(part == 0, high, jnp.where(part == 1, middle, low)).astype(bf16)


def body(
    near,
    far,
    charges_hbm,
    coords_hbm,
    areas_hbm,
    col_hbm,
    row_hbm,
    up_hbm,
    down_hbm,
    coupling_hbm,
    up_tr_hbm,
    down_tr_hbm,
    sibling_hbm,
    branch_hbm,
    out,
    charges,
    coords,
    areas,
    coef,
    col,
    rowb,
    leaf_up,
    leaf_down,
    coupling,
    up_tr,
    down_tr,
    sibling,
    branch,
    source,
    weight,
    target,
    node0,
    partner0,
    ynodes,
    nodes2,
    nodes3,
    xnodes,
    nodes5,
    roots,
    down0,
    local_sem,
    send_sem,
    recv_sem,
):
    b = lax.axis_index("branch")
    c = lax.axis_index("cluster")
    core = c % 2
    y = (c // 2) % NY
    x = c // (2 * NY)
    own = pl.ds(LEAVES, LEAVES)

    loads = []
    for source_ref, target_ref in (
        (charges_hbm, charges.at[own]),
        (col_hbm, col),
        (coords_hbm, coords.at[own]),
        (areas_hbm, areas.at[own]),
        (up_hbm, leaf_up),
        (up_tr_hbm, up_tr),
        (sibling_hbm, sibling),
        (down_tr_hbm, down_tr),
        (branch_hbm, branch),
        (coupling_hbm, coupling),
        (down_hbm, leaf_down),
        (row_hbm, rowb),
    ):
        copy = pltpu.make_async_copy(source_ref, target_ref, local_sem.at[len(loads)])
        copy.start()
        loads.append(copy)

    left = (b, (c + CLUSTERS - 1) % CLUSTERS)
    right = (b, (c + 1) % CLUSTERS)
    partner = (b, c + 1 - 2 * core)
    y_peers = [(b, (x * NY + (y + k) % NY) * 2 + core) for k in range(1, NY)]
    x_peers = [(b, (((x + k) % NX) * NY + y) * 2 + core) for k in range(1, NX)]
    z_peers = [((b + k) % NZ, c) for k in range(1, NZ)]

    barrier = pltpu.get_barrier_semaphore()
    everyone = [left, right] + y_peers + x_peers + z_peers
    for peer in everyone:
        pl.semaphore_signal(barrier, inc=1, device_id=peer, device_id_type=MESH)

    def remote(source_ref, target_ref, index, peer):
        return pltpu.make_async_remote_copy(
            src_ref=source_ref,
            dst_ref=target_ref,
            send_sem=send_sem.at[index],
            recv_sem=recv_sem.at[index],
            device_id=peer,
            device_id_type=MESH,
        )

    low_side, high_side = pl.ds(0, LEAVES), pl.ds(2 * LEAVES, LEAVES)

    def neighbour_copies(ref, index):
        return [
            remote(ref.at[own], ref.at[high_side], index, left),
            remote(ref.at[own], ref.at[low_side], index + 1, right),
        ]

    raw = neighbour_copies(coords, 0) + neighbour_copies(areas, 2) + neighbour_copies(charges, 4)
    coefs = neighbour_copies(coef, 6)
    to_partner = remote(node0, partner0, 8, partner)
    to_y = [remote(ynodes.at[y], ynodes.at[y], 9 + k, peer) for k, peer in enumerate(y_peers)]
    to_x = [remote(xnodes.at[x], xnodes.at[x], 16 + k, peer) for k, peer in enumerate(x_peers)]
    to_z = [remote(roots.at[b], roots.at[b], 19 + k, peer) for k, peer in enumerate(z_peers)]

    loads[0].wait()
    loads[1].wait()

    @pl.loop(0, LEAVES // 4)
    def _(step):
        for inner in range(4):
            n = step * 4 + inner
            coef[LEAVES + n] = dot3(charges[LEAVES + n], col[n])

    for index in (2, 3, 4, 5):
        loads[index].wait()
    pl.semaphore_wait(barrier, len(everyone))
    for copy in raw + coefs:
        copy.start()

    def add_leaf(step, total):
        for inner in range(4):
            n = step * 4 + inner
            total = total + dot3(coef[LEAVES + n], leaf_up[n])
        return total

    node0[...] = lax.fori_loop(0, LEAVES // 4, add_leaf, jnp.zeros((SCEN, RANK), f32))
    to_partner.start()

    total = coords[LEAVES]
    for n in range(1, LEAVES):
        total = total + coords[LEAVES + n]
    centre = jnp.sum(total, axis=1, keepdims=True) * (1.0 / (LEAVES * PANELS))

    def prepare(m):
        source[m] = features(coords[m] - centre, True)
        scaled = charges[m] * (areas[pl.ds(m, 1)] * inv_four_pi)
        high, low = halves(scaled)
        weight[m, 0:SCEN] = high
        weight[m, SCEN : 2 * SCEN] = low

    @pl.loop(0, LEAVES // 2)
    def _(step):
        for inner in range(2):
            n = step * 2 + inner
            prepare(LEAVES + n)
            target[n] = features(coords[LEAVES + n] - centre, False)

    def pair_up(level, left_child, right_child):
        return dot3(left_child, up_tr[level, 0]) + dot3(right_child, up_tr[level, 1])

    def rows(nodes, picks):
        parts = [nodes[SCEN * i : SCEN * i + SCEN] for i in picks]
        return parts[0] if len(parts) == 1 else jnp.concatenate(parts, axis=0)

    to_partner.wait()
    mine, other = node0[...], partner0[...]
    even = core == 0
    ynodes[y] = pair_up(0, jnp.where(even, mine, other), jnp.where(even, other, mine))
    for copy in to_y:
        copy.start()
    for copy in raw:
        copy.wait()

    @pl.loop(0, LEAVES // 2)
    def _(step):
        for inner in range(2):
            n = step * 2 + inner
            prepare(n)
            prepare(2 * LEAVES + n)

    def phase_y():
        for copy in to_y:
            copy.wait()
        level = jnp.concatenate([ynodes[i] for i in range(NY)], axis=0)
        level = pair_up(1, rows(level, (0, 2, 4, 6)), rows(level, (1, 3, 5, 7)))
        for i in range(4):
            nodes2[i] = rows(level, (i,))
        level = pair_up(2, rows(level, (0, 2)), rows(level, (1, 3)))
        for i in range(2):
            nodes3[i] = rows(level, (i,))
        xnodes[x] = pair_up(3, rows(level, (0,)), rows(level, (1,)))
        for copy in to_x:
            copy.start()

    def phase_x():
        for copy in to_x:
            copy.wait()
        level = jnp.concatenate([xnodes[i] for i in range(NX)], axis=0)
        level = pair_up(4, rows(level, (0, 2)), rows(level, (1, 3)))
        for i in range(2):
            nodes5[i] = rows(level, (i,))
        roots[b] = pair_up(5, rows(level, (0,)), rows(level, (1,)))
        for copy in to_z:
            copy.start()

    def flipped(index):
        return index + 1 - 2 * (index % 2)

    def phase_z():
        siblings = (
            partner0[...],
            ynodes[flipped(y)],
            nodes2[flipped(y // 2)],
            nodes3[flipped(y // 4)],
            xnodes[flipped(x)],
            nodes5[flipped(x // 2)],
        )
        sides = (core, y % 2, (y // 2) % 2, y // 4, x % 2, x // 2)
        parts = [dot3(siblings[level], sibling[level, sides[level]]) for level in range(LEVELS)]
        for copy in to_z:
            copy.wait()
        down = jnp.zeros((SCEN, RANK), f32)
        for i in range(NZ - 1):
            down = down + dot3(roots[(b + 1 + i) % NZ], branch[i])
        for level in reversed(range(LEVELS)):
            down = parts[level] + dot3(down, down_tr[level, sides[level]])
        down0[...] = down

    shift = LEAVES - (b * CLUSTERS + c) * LEAVES

    def window_index(leaf):
        return jnp.minimum(jnp.maximum(leaf + shift, 0), 3 * LEAVES - 1)

    @pl.loop(0, LEAVES)
    def _(n):
        tn = target[n]
        high_sum = jnp.zeros((2 * SCEN, PANELS), f32)
        low_sum = jnp.zeros((SCEN, PANELS), f32)
        for slot in range(NEAR):
            m = window_index(near[n, slot])
            kernel = lax.rsqrt(dot(source[m], tn, 0, 0))
            kernel_high, kernel_low = halves(kernel)
            wm = weight[m]
            high_sum = high_sum + dot(wm, kernel_high, 1, 0)
            low_sum = low_sum + dot(wm[:SCEN], kernel_low, 1, 0)
        out[n] = high_sum[:SCEN] + high_sum[SCEN:] + low_sum

        @pl.when(n == 0)
        def _():
            for index in range(6, 12):
                loads[index].wait()
            phase_y()

        @pl.when(n == 2)
        def _():
            phase_x()

        @pl.when(n == 5)
        def _():
            phase_z()

    for copy in coefs:
        copy.wait()

    down = down0[...]

    @pl.loop(0, LEAVES // 2)
    def _(step):
        for inner in range(2):
            n = step * 2 + inner
            total = dot3(down, leaf_down[n])
            for slot in range(FAR):
                total = total + dot3(coef[window_index(far[n, slot])], coupling[n, slot])
            out[n] = out[n] + dot3(total, rowb[n], 0)


def on_device(charges, coords, areas, col, row, up, down, coupling, up_tr, down_tr, sib, branch, near, far):
    window = 3 * LEAVES
    hbm = pl.BlockSpec(memory_space=pl.ANY)
    smem = pl.BlockSpec(memory_space=pltpu.SMEM)
    node = (SCEN, RANK)
    square = (RANK, RANK)
    copies = 26
    return pl.pallas_call(
        body,
        out_shape=jax.ShapeDtypeStruct((LEAVES, SCEN, PANELS), f32),
        in_specs=[smem] * 2 + [hbm] * 12,
        out_specs=pl.BlockSpec(memory_space=pltpu.VMEM),
        scratch_shapes=[
            pltpu.VMEM((window, SCEN, PANELS), f32),
            pltpu.VMEM((window, 3, PANELS), f32),
            pltpu.VMEM((window, PANELS), f32),
            pltpu.VMEM((window,) + node, f32),
            pltpu.VMEM((LEAVES, RANK, PANELS), f32),
            pltpu.VMEM((LEAVES, RANK, PANELS), f32),
            pltpu.VMEM((LEAVES,) + square, f32),
            pltpu.VMEM((LEAVES,) + square, f32),
            pltpu.VMEM((LEAVES, FAR) + square, f32),
            pltpu.VMEM((LEVELS, 2) + square, f32),
            pltpu.VMEM((LEVELS, 2) + square, f32),
            pltpu.VMEM((LEVELS, 2) + square, f32),
            pltpu.VMEM((NZ - 1,) + square, f32),
            pltpu.VMEM((window, FEATURES, PANELS), bf16),
            pltpu.VMEM((window, 2 * SCEN, PANELS), bf16),
            pltpu.VMEM((LEAVES, FEATURES, PANELS), bf16),
            pltpu.VMEM(node, f32),
            pltpu.VMEM(node, f32),
            pltpu.VMEM((NY,) + node, f32),
            pltpu.VMEM((4,) + node, f32),
            pltpu.VMEM((2,) + node, f32),
            pltpu.VMEM((NX,) + node, f32),
            pltpu.VMEM((2,) + node, f32),
            pltpu.VMEM((NZ,) + node, f32),
            pltpu.VMEM(node, f32),
            pltpu.SemaphoreType.DMA((12,)),
            pltpu.SemaphoreType.DMA((copies,)),
            pltpu.SemaphoreType.DMA((copies,)),
        ],
        compiler_params=pltpu.CompilerParams(
            collective_id=0, has_side_effects=True, vmem_limit_bytes=48 << 20
        ),
        name="hmatvec",
    )(near, far, charges, coords, areas, col, row, up, down, coupling, up_tr[0], down_tr[0], sib[0], branch[0])


def solution(mesh):
    leaf = ("branch", "cluster")

    def spec(axis, rank):
        return P(axis, *([None] * (rank - 1)))

    in_specs = (
        spec(leaf, 3),
        spec(leaf, 3),
        spec(leaf, 2),
        spec(leaf, 3),
        spec(leaf, 3),
        spec(leaf, 3),
        spec(leaf, 3),
        spec(leaf, 4),
        spec("branch", 5),
        spec("branch", 5),
        spec("branch", 5),
        spec("branch", 4),
        spec(leaf, 2),
        spec(leaf, 2),
    )
    return jax.shard_map(
        on_device, mesh=mesh, in_specs=in_specs, out_specs=spec(leaf, 3), check_vma=False
    )
```

time: 268 us -> 73.2 us (0.27)
  the two profiles are of different devices: /device:TPU:4 before, /device:TPU:8 now
where the time goes in v1:
time: 73.2 us; the launch traced here: 72.6 us
  Pallas kernels  59.4 us (81%)
  local copies, waits for them, and re-layouts  13.1 us (18%)
    pallas_call x1, Pallas kernels, on_device(): pl.pallas_call(body, out_shape=jax.ShapeDtypeStruct((LEAVES, SCEN, PANELS...  59.4 us
    unnamed x25, local copies, waits for them, and re-layouts  13.1 us

profile of v1, /device:TPU:8, one launch (start us, length us, event | category | flops | bytes accessed | tf_op | source)
XLA Modules:
  0.0 72.6 jit_solution(10975589293828154925)
XLA Ops:
  0.0 0.8 %copy.15.far = s32[16,4]{1,0:T(8,128)S(1)} copy(s32[16,4]{0,1:T(4,128)} %param.27) | data formatting | bytes 512 | tf_op args[13]
  0.8 0.8 %copy.16.coords_hbm = f32[16,3,256]{2,1,0:T(4,128)S(1)} copy(f32[16,3,256]{2,0,1:T(8,128)} %param.15) | data formatting | bytes 98304 | tf_op args[1]
  1.6 0.0 copy-start
  1.6 1.2 %copy-done = f32[16,64,256]{2,1,0:T(8,128)S(1)} copy-done((f32[16,64,256]{2,1,0:T(8,128)S(1)}, f32[16,64,256]{2,1,0:T(8,128)}, u32[]{:S(2)}) %copy-start) | copy-done | bytes 1048600
  2.8 0.0 copy-start.1
  2.8 1.2 %copy-done.1 = f32[16,64,256]{2,1,0:T(8,128)S(1)} copy-done((f32[16,64,256]{2,1,0:T(8,128)S(1)}, f32[16,64,256]{2,1,0:T(8,128)}, u32[]{:S(2)}) %copy-start.1) | copy-done | bytes 1048600
  4.0 0.0 copy-start.2
  4.1 1.0 %copy-done.2 = f32[16,64,64]{2,1,0:T(8,128)S(1)} copy-done((f32[16,64,64]{2,1,0:T(8,128)S(1)}, f32[16,64,64]{2,1,0:T(8,128)}, u32[]{:S(2)}) %copy-start.2) | copy-done | bytes 262168
  5.1 0.0 copy-start.3
  5.1 1.0 %copy-done.3 = f32[16,64,64]{2,1,0:T(8,128)S(1)} copy-done((f32[16,64,64]{2,1,0:T(8,128)S(1)}, f32[16,64,64]{2,1,0:T(8,128)}, u32[]{:S(2)}) %copy-start.3) | copy-done | bytes 262168
  6.1 0.0 copy-start.4
  6.1 1.0 %copy-done.4 = f32[1,6,2,64,64]{4,3,2,1,0:T(8,128)S(1)} copy-done((f32[1,6,2,64,64]{4,3,2,1,0:T(8,128)S(1)}, f32[1,6,2,64,64]{4,3,2,1,0:T(8,128)}, u32[]{:S(2)}) %copy-start.4) | copy-done | bytes 196632
  7.1 0.0 copy-start.5
  7.1 1.0 %copy-done.5 = f32[1,6,2,64,64]{4,3,2,1,0:T(8,128)S(1)} copy-done((f32[1,6,2,64,64]{4,3,2,1,0:T(8,128)S(1)}, f32[1,6,2,64,64]{4,3,2,1,0:T(8,128)}, u32[]{:S(2)}) %copy-start.5) | copy-done | bytes 196632
  8.1 0.0 copy-start.6
  8.1 1.0 %copy-done.6 = f32[1,6,2,64,64]{4,3,2,1,0:T(8,128)S(1)} copy-done((f32[1,6,2,64,64]{4,3,2,1,0:T(8,128)S(1)}, f32[1,6,2,64,64]{4,3,2,1,0:T(8,128)}, u32[]{:S(2)}) %copy-start.6) | copy-done | bytes 196632
  9.1 0.0 copy-start.7
  9.1 0.9 %copy-done.7 = f32[16,16,256]{2,1,0:T(8,128)S(1)} copy-done((f32[16,16,256]{2,1,0:T(8,128)S(1)}, f32[16,16,256]{2,1,0:T(8,128)}, u32[]{:S(2)}) %copy-start.7) | copy-done | bytes 262168
  10.1 0.0 copy-start.8
  10.1 0.9 %copy-done.8 = f32[1,7,64,64]{3,2,1,0:T(8,128)S(1)} copy-done((f32[1,7,64,64]{3,2,1,0:T(8,128)S(1)}, f32[1,7,64,64]{3,2,1,0:T(8,128)}, u32[]{:S(2)}) %copy-start.8) | copy-done | bytes 114712
  11.0 0.7 copy-done.9
  11.7 0.7 copy-done.10
  12.4 59.4 %hmatvec.1 = f32[16,16,256]{2,1,0:T(8,128)S(1)} custom-call(s32[16,16]{1,0:T(8,128)S(1)} %copy-done.10, s32[16,4]{1,0:T(8,128)S(1)} %copy.15.far, f32[16,16,256]{2,1,0:T(8,128)S(1)} %copy-done.7, f32[16,3,256]{2,1,0:T(4,128)S(1)} %copy.16.coords_hbm, f32[16,256]{1,0:T(8,128)S(1)} %copy-done.9, f32[16,64,256]{2,1,0:T(8,128)S(1)} %copy-done, ...), custom_call_target="tpu_custom_call" | custom-call | tf_op jit(solution)/shard_map/hmatvec/pallas_call | solution.py:342
  71.9 0.7 copy.18
  (2 shorter events, 0.0 us)
Async XLA Ops:
  1.6 1.2 %copy-start = (f32[16,64,256]{2,1,0:T(8,128)S(1)}, f32[16,64,256]{2,1,0:T(8,128)}, u32[]{:S(2)}) copy-start(f32[16,64,256]{2,1,0:T(8,128)} %col_hbm.1) | copy-start | bytes 3145732
  2.8 1.2 %copy-start.1 = (f32[16,64,256]{2,1,0:T(8,128)S(1)}, f32[16,64,256]{2,1,0:T(8,128)}, u32[]{:S(2)}) copy-start(f32[16,64,256]{2,1,0:T(8,128)} %row_hbm.1) | copy-start | bytes 3145732
  4.0 1.0 %copy-start.2 = (f32[16,64,64]{2,1,0:T(8,128)S(1)}, f32[16,64,64]{2,1,0:T(8,128)}, u32[]{:S(2)}) copy-start(f32[16,64,64]{2,1,0:T(8,128)} %up_hbm.1) | copy-start | bytes 786436
  5.1 1.0 %copy-start.3 = (f32[16,64,64]{2,1,0:T(8,128)S(1)}, f32[16,64,64]{2,1,0:T(8,128)}, u32[]{:S(2)}) copy-start(f32[16,64,64]{2,1,0:T(8,128)} %down_hbm.1) | copy-start | bytes 786436
  6.1 1.0 %copy-start.4 = (f32[1,6,2,64,64]{4,3,2,1,0:T(8,128)S(1)}, f32[1,6,2,64,64]{4,3,2,1,0:T(8,128)}, u32[]{:S(2)}) copy-start(f32[1,6,2,64,64]{4,3,2,1,0:T(8,128)} %param.22) | copy-start | bytes 589828
  7.1 1.0 %copy-start.5 = (f32[1,6,2,64,64]{4,3,2,1,0:T(8,128)S(1)}, f32[1,6,2,64,64]{4,3,2,1,0:T(8,128)}, u32[]{:S(2)}) copy-start(f32[1,6,2,64,64]{4,3,2,1,0:T(8,128)} %param.23) | copy-start | bytes 589828
  8.1 1.0 %copy-start.6 = (f32[1,6,2,64,64]{4,3,2,1,0:T(8,128)S(1)}, f32[1,6,2,64,64]{4,3,2,1,0:T(8,128)}, u32[]{:S(2)}) copy-start(f32[1,6,2,64,64]{4,3,2,1,0:T(8,128)} %param.24) | copy-start | bytes 589828
  9.1 0.9 %copy-start.7 = (f32[16,16,256]{2,1,0:T(8,128)S(1)}, f32[16,16,256]{2,1,0:T(8,128)}, u32[]{:S(2)}) copy-start(f32[16,16,256]{2,1,0:T(8,128)} %charges_hbm.1) | copy-start | bytes 786436
  10.1 0.9 %copy-start.8 = (f32[1,7,64,64]{3,2,1,0:T(8,128)S(1)}, f32[1,7,64,64]{3,2,1,0:T(8,128)}, u32[]{:S(2)}) copy-start(f32[1,7,64,64]{3,2,1,0:T(8,128)} %param.25) | copy-start | bytes 344068
  11.0 0.7 copy-start.9
  11.7 0.7 copy-start.10

commit v2 on v1

v2 whole, which is shorter than its diff:
```python
import functools
import math

import jax
import jax.numpy as jnp
from jax import lax
from jax.experimental import pallas as pl
from jax.experimental.pallas import tpu as pltpu
from jax.sharding import PartitionSpec as P

f32, bf16 = jnp.float32, jnp.bfloat16
MESH = pl.DeviceIdType.MESH
reg_square = 0.01
inv_four_pi = 0.25 / math.pi

LEAVES, SCEN, PANELS, RANK = 16, 16, 256, 64
NEAR, FAR, LEVELS = 16, 4, 6
NX, NY, NZ, CLUSTERS = 4, 8, 8, 64
FEATURES = 32
BARRIER_AT = 5
PAIRS = ((0, 0), (0, 1), (1, 0), (0, 2), (2, 0), (1, 1), (1, 2), (2, 1))


def dot(a, b, ca, cb):
    return lax.dot_general(a, b, (((ca,), (cb,)), ((), ())), preferred_element_type=f32)


def halves(x):
    high = x.astype(bf16)
    return high, (x - high.astype(f32)).astype(bf16)


def split_dot(a, b, ca, cb):
    return dot(a[0], b[0], ca, cb) + dot(a[1], b[0], ca, cb) + dot(a[0], b[1], ca, cb)


def dot3(a, b, cb=1):
    return split_dot(halves(a), halves(b), 1, cb)


def features(x, y, z, is_source):
    row = lax.broadcasted_iota(jnp.int32, (FEATURES, PANELS), 0)
    dim = row % 3
    coord_row = row < 24
    x, y, z = (jnp.broadcast_to(value, (FEATURES, PANELS)) for value in (x, y, z))
    square = x * x + y * y + z * z
    value = jnp.where(dim == 0, x, jnp.where(dim == 1, y, z))
    pair = row // 3
    part = jnp.zeros_like(row)
    side = 0 if is_source else 1
    for index, parts in enumerate(PAIRS):
        if parts[side]:
            part = jnp.where(pair == index, parts[side], part)
    if is_source:
        value = jnp.where(coord_row, value, jnp.where(pair == 8, square, 1.0))
        part = jnp.where(pair == 8, dim, part)
    else:
        value = jnp.where(coord_row, -2.0 * value, jnp.where(pair == 8, 1.0, square + reg_square))
        part = jnp.where(pair == 9, dim, part)
    value = jnp.where(row < 30, value, 0.0)
    high = value.astype(bf16).astype(f32)
    rest = value - high
    middle = rest.astype(bf16).astype(f32)
    low = rest - middle
    return jnp.where(part == 0, high, jnp.where(part == 1, middle, low)).astype(bf16)


def place():
    b = lax.axis_index("branch")
    c = lax.axis_index("cluster")
    return b, c, c % 2, (c // 2) % NY, c // (2 * NY)


def remote(source_ref, target_ref, send_sem, recv_sem, index, peer):
    return pltpu.make_async_remote_copy(
        src_ref=source_ref,
        dst_ref=target_ref,
        send_sem=send_sem.at[index],
        recv_sem=recv_sem.at[index],
        device_id=peer,
        device_id_type=MESH,
    )


def greet(peers):
    barrier = pltpu.get_barrier_semaphore()
    for peer in peers:
        pl.semaphore_signal(barrier, inc=1, device_id=peer, device_id_type=MESH)
    return lambda: pl.semaphore_wait(barrier, len(peers))


def start_loads(pairs, sem):
    copies = [pltpu.make_async_copy(a, b, sem.at[i]) for i, (a, b) in enumerate(pairs)]
    for copy in copies:
        copy.start()
    return copies


def flipped(index):
    return index + 1 - 2 * (index % 2)


def exchange(
    charges_hbm,
    coords_hbm,
    areas_hbm,
    col_hbm,
    up_hbm,
    up_tr_hbm,
    coupling_hbm,
    down_hbm,
    row_hbm,
    sibling_hbm,
    far_hbm,
    source_out,
    weight_out,
    target_out,
    base_out,
    high_out,
    low_out,
    root_out,
    parts_out,
    charges,
    coords,
    areas,
    coef,
    col,
    rowb,
    leaf_up,
    leaf_down,
    coupling,
    up_tr,
    sibling,
    far,
    source,
    weight,
    target,
    base,
    down_high,
    down_low,
    node0,
    partner0,
    ynodes,
    nodes2,
    nodes3,
    xnodes,
    nodes5,
    root,
    parts,
    local_sem,
    out_sem,
    send_sem,
    recv_sem,
):
    b, c, core, y, x = place()
    own = pl.ds(LEAVES, LEAVES)
    low_side, high_side = pl.ds(0, LEAVES), pl.ds(2 * LEAVES, LEAVES)
    left = (b, (c + CLUSTERS - 1) % CLUSTERS)
    right = (b, (c + 1) % CLUSTERS)
    partner = (b, flipped(c))
    y_peers = [(b, (x * NY + (y + k) % NY) * 2 + core) for k in range(1, NY)]
    x_peers = [(b, (((x + k) % NX) * NY + y) * 2 + core) for k in range(1, NX)]
    wait_for_all = greet([left, right] + y_peers + x_peers)

    loads = start_loads(
        (
            (coords_hbm, coords.at[:, own]),
            (areas_hbm, areas.at[own]),
            (charges_hbm, charges.at[own]),
            (col_hbm, col),
            (up_hbm, leaf_up),
            (up_tr_hbm, up_tr),
            (coupling_hbm, coupling),
            (row_hbm, rowb),
            (down_hbm, leaf_down),
            (sibling_hbm, sibling),
            (far_hbm, far),
        ),
        local_sem,
    )

    def send(source_ref, target_ref, index, peer):
        return remote(source_ref, target_ref, send_sem, recv_sem, index, peer)

    def sides(ref, index, lead):
        at = (lambda part: ref.at[:, part]) if lead else (lambda part: ref.at[part])
        return [send(at(own), at(high_side), index, left), send(at(own), at(low_side), index + 1, right)]

    coords_copies = sides(coords, 0, True)
    areas_copies = sides(areas, 2, False)
    charges_copies = sides(charges, 4, False)
    coef_copies = sides(coef, 6, False)
    to_partner = send(node0, partner0, 8, partner)
    to_y = [send(ynodes.at[y], ynodes.at[y], 9 + k, peer) for k, peer in enumerate(y_peers)]
    to_x = [send(xnodes.at[x], xnodes.at[x], 16 + k, peer) for k, peer in enumerate(x_peers)]

    for index in range(3):
        loads[index].wait()
    wait_for_all()
    for copy in coords_copies + areas_copies + charges_copies:
        copy.start()

    loads[3].wait()

    @pl.loop(0, LEAVES // 8)
    def _(step):
        for inner in range(8):
            n = step * 8 + inner
            coef[LEAVES + n] = dot3(charges[LEAVES + n], col[n])

    for copy in coef_copies:
        copy.start()
    loads[4].wait()

    def add_leaf(step, total):
        for inner in range(8):
            n = step * 8 + inner
            total = total + dot3(coef[LEAVES + n], leaf_up[n])
        return total

    node0[...] = lax.fori_loop(0, LEAVES // 8, add_leaf, jnp.zeros((SCEN, RANK), f32))
    to_partner.start()

    centres = []
    for i in range(3):
        mean = jnp.sum(coords[i, LEAVES : 2 * LEAVES], axis=0, keepdims=True)
        centres.append(jnp.sum(mean, axis=1, keepdims=True) * (1.0 / (LEAVES * PANELS)))

    def features_of(m, is_source):
        point = [coords[i, pl.ds(m, 1)] - centres[i] for i in range(3)]
        return features(*point, is_source)

    def weigh(m):
        high, low = halves(charges[m] * (areas[pl.ds(m, 1)] * inv_four_pi))
        weight[m, 0:SCEN] = high
        weight[m, SCEN : 2 * SCEN] = low

    @pl.loop(0, LEAVES // 2)
    def _(step):
        for inner in range(2):
            n = step * 2 + inner
            source[LEAVES + n] = features_of(LEAVES + n, True)
            target[n] = features_of(LEAVES + n, False)
            weigh(LEAVES + n)

    def pair_up(level, left_child, right_child):
        return dot3(left_child, up_tr[level, 0]) + dot3(right_child, up_tr[level, 1])

    def rows(nodes, picks):
        found = [nodes[SCEN * i : SCEN * i + SCEN] for i in picks]
        return found[0] if len(found) == 1 else jnp.concatenate(found, axis=0)

    loads[5].wait()
    to_partner.wait()
    mine, other = node0[...], partner0[...]
    even = core == 0
    ynodes[y] = pair_up(0, jnp.where(even, mine, other), jnp.where(even, other, mine))
    for copy in to_y:
        copy.start()

    for copy in coords_copies:
        copy.wait()

    @pl.loop(0, LEAVES // 2)
    def _(step):
        for inner in range(2):
            n = step * 2 + inner
            source[n] = features_of(n, True)
            source[2 * LEAVES + n] = features_of(2 * LEAVES + n, True)

    stores = [
        pltpu.make_async_copy(ref, hbm, out_sem.at[i])
        for i, (ref, hbm) in enumerate(
            (
                (source, source_out),
                (target, target_out),
                (weight, weight_out),
                (base, base_out),
                (down_high, high_out),
                (down_low, low_out),
                (root, root_out),
                (parts, parts_out),
            )
        )
    ]
    stores[0].start()
    stores[1].start()

    for copy in to_y:
        copy.wait()
    level = jnp.concatenate([ynodes[i] for i in range(NY)], axis=0)
    level = pair_up(1, rows(level, (0, 2, 4, 6)), rows(level, (1, 3, 5, 7)))
    for i in range(4):
        nodes2[i] = rows(level, (i,))
    level = pair_up(2, rows(level, (0, 2)), rows(level, (1, 3)))
    for i in range(2):
        nodes3[i] = rows(level, (i,))
    xnodes[x] = pair_up(3, rows(level, (0,)), rows(level, (1,)))
    for copy in to_x:
        copy.start()

    for copy in areas_copies + charges_copies:
        copy.wait()

    @pl.loop(0, LEAVES // 4)
    def _(step):
        for inner in range(4):
            n = step * 4 + inner
            weigh(n)
            weigh(2 * LEAVES + n)

    stores[2].start()

    for index in range(6, 11):
        loads[index].wait()
    for copy in coef_copies:
        copy.wait()
    shift = LEAVES - (b * CLUSTERS + c) * LEAVES

    @pl.loop(0, LEAVES // 2)
    def _(step):
        for inner in range(2):
            n = step * 2 + inner
            total = jnp.zeros((SCEN, RANK), f32)
            for slot in range(FAR):
                m = jnp.minimum(jnp.maximum(far[slot, n] + shift, 0), 3 * LEAVES - 1)
                total = total + dot3(coef[m], coupling[n, slot])
            row_halves = halves(rowb[n])
            base[n] = split_dot(halves(total), row_halves, 1, 0)
            down_high[n], down_low[n] = halves(split_dot(halves(leaf_down[n]), row_halves, 0, 0))

    for index in range(3, 6):
        stores[index].start()

    for copy in to_x:
        copy.wait()
    level = jnp.concatenate([xnodes[i] for i in range(NX)], axis=0)
    level = pair_up(4, rows(level, (0, 2)), rows(level, (1, 3)))
    for i in range(2):
        nodes5[i] = rows(level, (i,))
    root[...] = pair_up(5, rows(level, (0,)), rows(level, (1,)))
    stores[6].start()
    siblings = (
        partner0[...],
        ynodes[flipped(y)],
        nodes2[flipped(y // 2)],
        nodes3[flipped(y // 4)],
        xnodes[flipped(x)],
        nodes5[flipped(x // 2)],
    )
    for index, side in enumerate((core, y % 2, (y // 2) % 2, y // 4, x % 2, x // 2)):
        parts[index] = dot3(siblings[index], sibling[index, side])
    stores[7].start()
    for copy in stores:
        copy.wait()


def near_field(
    near_hbm,
    source_hbm,
    target_hbm,
    weight_hbm,
    base_hbm,
    high_hbm,
    low_hbm,
    root_hbm,
    parts_hbm,
    down_tr_hbm,
    branch_hbm,
    out,
    near,
    source,
    target,
    weight,
    base,
    down_high,
    down_low,
    roots,
    parts,
    down_tr,
    branch,
    local_sem,
    send_sem,
    recv_sem,
):
    b, c, core, y, x = place()
    z_peers = [((b + k) % NZ, c) for k in range(1, NZ)]
    wait_for_all = greet(z_peers)
    loads = start_loads(
        (
            (near_hbm, near),
            (target_hbm, target),
            (source_hbm, source),
            (weight_hbm, weight),
            (base_hbm, base),
            (root_hbm, roots.at[b]),
            (high_hbm, down_high),
            (low_hbm, down_low),
            (parts_hbm, parts),
            (down_tr_hbm, down_tr),
            (branch_hbm, branch),
        ),
        local_sem,
    )
    to_z = [
        remote(roots.at[b], roots.at[b], send_sem, recv_sem, k, peer) for k, peer in enumerate(z_peers)
    ]
    for index in range(5):
        loads[index].wait()
    shift = LEAVES - (b * CLUSTERS + c) * LEAVES

    @pl.loop(0, LEAVES)
    def _(n):
        tn = target[n]
        high_sum = jnp.zeros((2 * SCEN, PANELS), f32)
        low_sum = jnp.zeros((SCEN, PANELS), f32)
        for slot in range(NEAR):
            m = jnp.minimum(jnp.maximum(near[n, slot] + shift, 0), 3 * LEAVES - 1)
            kernel = lax.rsqrt(dot(source[m], tn, 0, 0))
            kernel_high, kernel_low = halves(kernel)
            wm = weight[m]
            high_sum = high_sum + dot(wm, kernel_high, 1, 0)
            low_sum = low_sum + dot(wm[:SCEN], kernel_low, 1, 0)
        out[n] = base[n] + (high_sum[:SCEN] + high_sum[SCEN:] + low_sum)

        @pl.when(n == BARRIER_AT)
        def _():
            wait_for_all()
            loads[5].wait()
            for copy in to_z:
                copy.start()

    for index in range(6, 11):
        loads[index].wait()
    for copy in to_z:
        copy.wait()
    down = jnp.zeros((SCEN, RANK), f32)
    for i in range(NZ - 1):
        down = down + dot3(roots[(b + 1 + i) % NZ], branch[i])
    side = (core, y % 2, (y // 2) % 2, y // 4, x % 2, x // 2)
    for level in reversed(range(LEVELS)):
        down = parts[level] + dot3(down, down_tr[level, side[level]])
    halved = halves(down)

    @pl.loop(0, LEAVES // 8)
    def _(step):
        for inner in range(8):
            n = step * 8 + inner
            out[n] = out[n] + split_dot(halved, (down_high[n], down_low[n]), 1, 0)


def on_device(charges, coords, areas, col, row, up, down, coupling, up_tr, down_tr, sib, branch, near, far):
    window = 3 * LEAVES
    hbm = pl.BlockSpec(memory_space=pltpu.HBM)
    node = (SCEN, RANK)
    square = (RANK, RANK)
    features_shape = (window, FEATURES, PANELS)
    weight_shape = (window, 2 * SCEN, PANELS)
    target_shape = (LEAVES, FEATURES, PANELS)
    leaf_shape = (LEAVES, SCEN, PANELS)
    down_shape = (LEAVES, RANK, PANELS)
    made = (
        (features_shape, bf16),
        (weight_shape, bf16),
        (target_shape, bf16),
        (leaf_shape, f32),
        (down_shape, bf16),
        (down_shape, bf16),
        (node, f32),
        ((LEVELS,) + node, f32),
    )

    def params(collective_id):
        return pltpu.CompilerParams(
            collective_id=collective_id, has_side_effects=True, vmem_limit_bytes=67043328
        )

    scratch = [pltpu.VMEM(shape, kind) for shape, kind in made]
    source, weight, target, base, high, low, root, parts = pl.pallas_call(
        exchange,
        out_shape=[jax.ShapeDtypeStruct(shape, kind) for shape, kind in made],
        in_specs=[hbm] * 11,
        out_specs=[hbm] * 8,
        scratch_shapes=[
            pltpu.VMEM((window, SCEN, PANELS), f32),
            pltpu.VMEM((3, window, PANELS), f32),
            pltpu.VMEM((window, PANELS), f32),
            pltpu.VMEM((window,) + node, f32),
            pltpu.VMEM((LEAVES, RANK, PANELS), f32),
            pltpu.VMEM((LEAVES, RANK, PANELS), f32),
            pltpu.VMEM((LEAVES,) + square, f32),
            pltpu.VMEM((LEAVES,) + square, f32),
            pltpu.VMEM((LEAVES, FAR) + square, f32),
            pltpu.VMEM((LEVELS, 2) + square, f32),
            pltpu.VMEM((LEVELS, 2) + square, f32),
            pltpu.SMEM((FAR, LEAVES), jnp.int32),
        ]
        + scratch[:6]
        + [
            pltpu.VMEM(node, f32),
            pltpu.VMEM(node, f32),
            pltpu.VMEM((NY,) + node, f32),
            pltpu.VMEM((4,) + node, f32),
            pltpu.VMEM((2,) + node, f32),
            pltpu.VMEM((NX,) + node, f32),
            pltpu.VMEM((2,) + node, f32),
        ]
        + scratch[6:]
        + [
            pltpu.SemaphoreType.DMA((11,)),
            pltpu.SemaphoreType.DMA((8,)),
            pltpu.SemaphoreType.DMA((19,)),
            pltpu.SemaphoreType.DMA((19,)),
        ],
        compiler_params=params(0),
        name="exchange",
    )(
        charges,
        jnp.transpose(coords, (1, 0, 2)),
        areas,
        col,
        up,
        up_tr[0],
        coupling,
        down,
        row,
        sib[0],
        far.T,
    )
    return pl.pallas_call(
        near_field,
        out_shape=jax.ShapeDtypeStruct(leaf_shape, f32),
        in_specs=[hbm] * 11,
        out_specs=pl.BlockSpec(memory_space=pltpu.VMEM),
        scratch_shapes=[
            pltpu.SMEM((LEAVES, NEAR), jnp.int32),
            scratch[0],
            scratch[2],
            scratch[1],
            scratch[3],
            scratch[4],
            scratch[5],
            pltpu.VMEM((NZ,) + node, f32),
            scratch[7],
            pltpu.VMEM((LEVELS, 2) + square, f32),
            pltpu.VMEM((NZ - 1,) + square, f32),
            pltpu.SemaphoreType.DMA((11,)),
            pltpu.SemaphoreType.DMA((NZ - 1,)),
            pltpu.SemaphoreType.DMA((NZ - 1,)),
        ],
        compiler_params=params(1),
        name="near_field",
    )(near, source, target, weight, base, high, low, root, parts, down_tr[0], branch[0])


def solution(mesh):
    leaf = ("branch", "cluster")

    def spec(axis, rank):
        return P(axis, *([None] * (rank - 1)))

    in_specs = (
        spec(leaf, 3),
        spec(leaf, 3),
        spec(leaf, 2),
        spec(leaf, 3),
        spec(leaf, 3),
        spec(leaf, 3),
        spec(leaf, 3),
        spec(leaf, 4),
        spec("branch", 5),
        spec("branch", 5),
        spec("branch", 5),
        spec("branch", 4),
        spec(leaf, 2),
        spec(leaf, 2),
    )
    return jax.shard_map(
        on_device, mesh=mesh, in_specs=in_specs, out_specs=spec(leaf, 3), check_vma=False
    )
```

time: 73.2 us -> 58.9 us (0.80)
  local copies, waits for them, and re-layouts: 13.1 us -> 1.67 us
  Pallas kernels: 59.4 us -> 57 us
    unnamed x25 -> x1, local copies, waits for them, and re-layouts: 13.1 us -> 1.67 us
    pallas_call x1 -> x2, Pallas kernels: 59.4 us -> 57 us  [the longest x1 29 us: on_device(): pl.pallas_call(near_field, out_shape=jax.ShapeDtypeStruct(leaf_shape, f32...]
where the time goes in v2:
time: 58.9 us; the launch traced here: 58.7 us
  Pallas kernels  57 us (97%)
  local copies, waits for them, and re-layouts  1.67 us (3%)
    pallas_call x1, Pallas kernels, on_device(): pl.pallas_call(near_field, out_shape=jax.ShapeDtypeStruct(leaf_shape, f32...  29 us
    pallas_call x1, Pallas kernels, on_device(): pl.pallas_call(exchange, out_shape=[jax.ShapeDtypeStruct(shape, kind) for...  28 us
    unnamed x1, local copies, waits for them, and re-layouts  1.67 us

profile of v2, /device:TPU:8, one launch (start us, length us, event | category | flops | bytes accessed | tf_op | source)
XLA Modules:
  0.0 58.7 jit_solution(18222130158124503483)
XLA Ops:
  0.0 28.0 %exchange.1 = (bf16[48,32,256]{2,1,0:T(8,128)(2,1)}, bf16[48,32,256]{2,1,0:T(8,128)(2,1)}, bf16[16,32,256]{2,1,0:T(8,128)(2,1)}, f32[16,16,256]{2,1,0:T(8,128)},...) custom-call(f32[16,16,256]{2,1,0:T(8,128)} %charges_hbm.1, ...), custom_call_target="tpu_custom_call" | custom-call | tf_op jit(solution)/shard_map/exchange/pallas_call | solution.py:479
  28.0 29.0 %near_field.1 = f32[16,16,256]{2,1,0:T(8,128)} custom-call(s32[16,16]{1,0:T(8,128)} %near_hbm.1, bf16[48,32,256]{2,1,0:T(8,128)(2,1)} %get-tuple-element.13.source_hbm, bf16[16,32,256]{2,1,0:T(8,128)(2,1)} %get-tuple-element.14.target_hbm, bf16[48,32,256]{2,1,0:T(8,128)(2,1)} %get-tuple-element.15.weight_hbm, f32[16,16,256]{2,1,0:T(8,128)} %get-tuple-element.16.base_hbm, ...), custom_call_target="tpu_custom_call" | custom-call | tf_op jit(solution)/shard_map/near_field/pallas_call | solution.py:530
  57.0 1.7 %copy.16 = f32[16,16,256]{2,1,0:T(8,128)} copy(f32[16,16,256]{2,1,0:T(8,128)} %near_field.1) | data formatting | bytes 524288

commit v3 on v2

v3 whole, which is shorter than its diff:
```python
import functools
import math

import jax
import jax.numpy as jnp
from jax import lax
from jax.experimental import pallas as pl
from jax.experimental.pallas import tpu as pltpu
from jax.sharding import PartitionSpec as P

f32, bf16 = jnp.float32, jnp.bfloat16
MESH = pl.DeviceIdType.MESH
reg_square = 0.01
inv_four_pi = 0.25 / math.pi

LEAVES, SCEN, PANELS, RANK = 16, 16, 256, 64
NEAR, FAR, LEVELS = 16, 4, 6
NX, NY, NZ, CLUSTERS = 4, 8, 8, 64
FEATURES = 32
FULL_VMEM = 67043328
BARRIER_AT, Y_AT, X_AT = 3, 6, 8
PAIRS = ((0, 0), (0, 1), (1, 0), (0, 2), (2, 0), (1, 1), (1, 2), (2, 1))


def dot(a, b, ca, cb):
    return lax.dot_general(a, b, (((ca,), (cb,)), ((), ())), preferred_element_type=f32)


def halves(x):
    high = x.astype(bf16)
    return high, (x - high.astype(f32)).astype(bf16)


def split_dot(a, b, ca, cb):
    rows = a[0].shape[1 - ca]
    both = dot(jnp.concatenate(a, axis=1 - ca), b[0], ca, cb)
    return both[:rows] + both[rows:] + dot(a[0], b[1], ca, cb)


def dot3(a, b, cb=1):
    return split_dot(halves(a), halves(b), 1, cb)


def features(x, y, z, is_source):
    row = lax.broadcasted_iota(jnp.int32, (FEATURES, PANELS), 0)
    dim = row % 3
    coord_row = row < 24
    x, y, z = (jnp.broadcast_to(value, (FEATURES, PANELS)) for value in (x, y, z))
    square = x * x + y * y + z * z
    value = jnp.where(dim == 0, x, jnp.where(dim == 1, y, z))
    pair = row // 3
    part = jnp.zeros_like(row)
    side = 0 if is_source else 1
    for index, parts in enumerate(PAIRS):
        if parts[side]:
            part = jnp.where(pair == index, parts[side], part)
    if is_source:
        value = jnp.where(coord_row, value, jnp.where(pair == 8, square, 1.0))
        part = jnp.where(pair == 8, dim, part)
    else:
        value = jnp.where(coord_row, -2.0 * value, jnp.where(pair == 8, 1.0, square + reg_square))
        part = jnp.where(pair == 9, dim, part)
    value = jnp.where(row < 30, value, 0.0)
    high = value.astype(bf16).astype(f32)
    rest = value - high
    middle = rest.astype(bf16).astype(f32)
    low = rest - middle
    return jnp.where(part == 0, high, jnp.where(part == 1, middle, low)).astype(bf16)


def place():
    b = lax.axis_index("branch")
    c = lax.axis_index("cluster")
    return b, c, c % 2, (c // 2) % NY, c // (2 * NY)


def remote(source_ref, target_ref, send_sem, recv_sem, index, peer):
    return pltpu.make_async_remote_copy(
        src_ref=source_ref,
        dst_ref=target_ref,
        send_sem=send_sem.at[index],
        recv_sem=recv_sem.at[index],
        device_id=peer,
        device_id_type=MESH,
    )


def greet(peers):
    barrier = pltpu.get_barrier_semaphore()
    for peer in peers:
        pl.semaphore_signal(barrier, inc=1, device_id=peer, device_id_type=MESH)
    return lambda: pl.semaphore_wait(barrier, len(peers))


def start_loads(pairs, sem):
    copies = [pltpu.make_async_copy(a, b, sem.at[i]) for i, (a, b) in enumerate(pairs)]
    for copy in copies:
        copy.start()
    return copies


def flipped(index):
    return index + 1 - 2 * (index % 2)


def pair_up(up_tr, level, left_child, right_child):
    return dot3(left_child, up_tr[level, 0]) + dot3(right_child, up_tr[level, 1])


def rows(nodes, picks):
    found = [nodes[SCEN * i : SCEN * i + SCEN] for i in picks]
    return found[0] if len(found) == 1 else jnp.concatenate(found, axis=0)


def exchange(
    charges_hbm,
    coords_hbm,
    areas_hbm,
    col_hbm,
    up_hbm,
    up_tr_hbm,
    source_out,
    weight_out,
    target_out,
    coef_out,
    pair_out,
    partner_out,
    charges,
    coords,
    areas,
    col,
    leaf_up,
    up_tr,
    node0,
    source,
    weight,
    target,
    coef,
    pair,
    partner0,
    local_sem,
    out_sem,
    send_sem,
    recv_sem,
):
    b, c, core, y, x = place()
    own = pl.ds(LEAVES, LEAVES)
    low_side, high_side = pl.ds(0, LEAVES), pl.ds(2 * LEAVES, LEAVES)
    left = (b, (c + CLUSTERS - 1) % CLUSTERS)
    right = (b, (c + 1) % CLUSTERS)
    partner = (b, flipped(c))
    wait_for_all = greet([left, right])

    loads = start_loads(
        (
            (coords_hbm, coords.at[:, own]),
            (areas_hbm, areas.at[own]),
            (charges_hbm, charges.at[own]),
            (col_hbm, col),
            (up_hbm, leaf_up),
            (up_tr_hbm, up_tr),
        ),
        local_sem,
    )

    def send(source_ref, target_ref, index, peer):
        return remote(source_ref, target_ref, send_sem, recv_sem, index, peer)

    def sides(ref, index, lead):
        at = (lambda part: ref.at[:, part]) if lead else (lambda part: ref.at[part])
        return [send(at(own), at(high_side), index, left), send(at(own), at(low_side), index + 1, right)]

    coords_copies = sides(coords, 0, True)
    areas_copies = sides(areas, 2, False)
    charges_copies = sides(charges, 4, False)
    coef_copies = sides(coef, 6, False)
    to_partner = send(node0, partner0, 8, partner)

    for index in range(3):
        loads[index].wait()
    wait_for_all()
    for copy in coords_copies + areas_copies + charges_copies:
        copy.start()

    loads[3].wait()

    @pl.loop(0, LEAVES // 8)
    def _(step):
        for inner in range(8):
            n = step * 8 + inner
            coef[LEAVES + n] = dot3(charges[LEAVES + n], col[n])

    for copy in coef_copies:
        copy.start()
    loads[4].wait()

    def add_leaf(step, total):
        for inner in range(8):
            n = step * 8 + inner
            total = total + dot3(coef[LEAVES + n], leaf_up[n])
        return total

    node0[...] = lax.fori_loop(0, LEAVES // 8, add_leaf, jnp.zeros((SCEN, RANK), f32))
    to_partner.start()

    centres = []
    for i in range(3):
        mean = jnp.sum(coords[i, LEAVES : 2 * LEAVES], axis=0, keepdims=True)
        centres.append(jnp.sum(mean, axis=1, keepdims=True) * (1.0 / (LEAVES * PANELS)))

    def features_of(m, is_source):
        point = [coords[i, pl.ds(m, 1)] - centres[i] for i in range(3)]
        return features(*point, is_source)

    def weigh(m):
        high, low = halves(charges[m] * (areas[pl.ds(m, 1)] * inv_four_pi))
        weight[m, 0:SCEN] = high
        weight[m, SCEN : 2 * SCEN] = low

    @pl.loop(0, LEAVES // 2)
    def _(step):
        for inner in range(2):
            n = step * 2 + inner
            source[LEAVES + n] = features_of(LEAVES + n, True)
            target[n] = features_of(LEAVES + n, False)
            weigh(LEAVES + n)

    parts = []

    def store(ref, hbm):
        copy = pltpu.make_async_copy(ref, hbm, out_sem.at[len(parts)])
        copy.start()
        parts.append(copy)

    store(target, target_out)
    store(source.at[own], source_out.at[own])
    store(weight.at[own], weight_out.at[own])

    loads[5].wait()
    to_partner.wait()
    mine, other = node0[...], partner0[...]
    even = core == 0
    pair[...] = pair_up(up_tr, 0, jnp.where(even, mine, other), jnp.where(even, other, mine))
    store(pair, pair_out)
    store(partner0, partner_out)

    for copy in coords_copies:
        copy.wait()

    @pl.loop(0, LEAVES // 2)
    def _(step):
        for inner in range(2):
            n = step * 2 + inner
            source[n] = features_of(n, True)
            source[2 * LEAVES + n] = features_of(2 * LEAVES + n, True)

    store(source.at[low_side], source_out.at[low_side])
    store(source.at[high_side], source_out.at[high_side])
    for copy in areas_copies + charges_copies:
        copy.wait()

    @pl.loop(0, LEAVES // 4)
    def _(step):
        for inner in range(4):
            n = step * 4 + inner
            weigh(n)
            weigh(2 * LEAVES + n)

    store(weight.at[low_side], weight_out.at[low_side])
    store(weight.at[high_side], weight_out.at[high_side])
    for copy in coef_copies:
        copy.wait()
    store(coef, coef_out)
    for copy in parts:
        copy.wait()


def near_field(
    near_hbm,
    far_hbm,
    source_hbm,
    target_hbm,
    weight_hbm,
    coef_hbm,
    pair_hbm,
    partner_hbm,
    coupling_hbm,
    down_hbm,
    row_hbm,
    up_tr_hbm,
    sibling_hbm,
    down_tr_hbm,
    branch_hbm,
    out,
    near,
    far,
    source,
    target,
    weight,
    coef,
    partner0,
    coupling,
    leaf_down,
    rowb,
    up_tr,
    sibling,
    down_tr,
    branch,
    local,
    down_high,
    down_low,
    ynodes,
    nodes2,
    nodes3,
    xnodes,
    nodes5,
    roots,
    local_sem,
    send_sem,
    recv_sem,
):
    b, c, core, y, x = place()
    y_peers = [(b, (x * NY + (y + k) % NY) * 2 + core) for k in range(1, NY)]
    x_peers = [(b, (((x + k) % NX) * NY + y) * 2 + core) for k in range(1, NX)]
    z_peers = [((b + k) % NZ, c) for k in range(1, NZ)]
    wait_for_all = greet(y_peers + x_peers + z_peers)
    loads = start_loads(
        (
            (near_hbm, near),
            (target_hbm, target),
            (source_hbm, source),
            (weight_hbm, weight),
            (pair_hbm, ynodes.at[y]),
            (up_tr_hbm, up_tr),
            (far_hbm, far),
            (coef_hbm, coef),
            (coupling_hbm, coupling),
            (row_hbm, rowb),
            (down_hbm, leaf_down),
            (partner_hbm, partner0),
            (sibling_hbm, sibling),
            (down_tr_hbm, down_tr),
            (branch_hbm, branch),
        ),
        local_sem,
    )

    def send(source_ref, target_ref, index, peer):
        return remote(source_ref, target_ref, send_sem, recv_sem, index, peer)

    to_y = [send(ynodes.at[y], ynodes.at[y], k, peer) for k, peer in enumerate(y_peers)]
    to_x = [send(xnodes.at[x], xnodes.at[x], 7 + k, peer) for k, peer in enumerate(x_peers)]
    to_z = [send(roots.at[b], roots.at[b], 10 + k, peer) for k, peer in enumerate(z_peers)]
    for index in range(4):
        loads[index].wait()
    shift = LEAVES - (b * CLUSTERS + c) * LEAVES

    def window_index(leaf):
        return jnp.minimum(jnp.maximum(leaf + shift, 0), 3 * LEAVES - 1)

    @pl.loop(0, LEAVES)
    def _(n):
        tn = target[n]
        high_sum = jnp.zeros((2 * SCEN, PANELS), f32)
        low_sum = jnp.zeros((SCEN, PANELS), f32)
        for slot in range(NEAR):
            m = window_index(near[n, slot])
            kernel = lax.rsqrt(dot(source[m], tn, 0, 0))
            kernel_high, kernel_low = halves(kernel)
            wm = weight[m]
            high_sum = high_sum + dot(wm, kernel_high, 1, 0)
            low_sum = low_sum + dot(wm[:SCEN], kernel_low, 1, 0)
        out[n] = high_sum[:SCEN] + high_sum[SCEN:] + low_sum

        @pl.when(n == BARRIER_AT)
        def _():
            loads[4].wait()
            loads[5].wait()
            wait_for_all()
            for copy in to_y:
                copy.start()

        @pl.when(n == Y_AT)
        def _():
            for copy in to_y:
                copy.wait()
            level = jnp.concatenate([ynodes[i] for i in range(NY)], axis=0)
            level = pair_up(up_tr, 1, rows(level, (0, 2, 4, 6)), rows(level, (1, 3, 5, 7)))
            for i in range(4):
                nodes2[i] = rows(level, (i,))
            level = pair_up(up_tr, 2, rows(level, (0, 2)), rows(level, (1, 3)))
            for i in range(2):
                nodes3[i] = rows(level, (i,))
            xnodes[x] = pair_up(up_tr, 3, rows(level, (0,)), rows(level, (1,)))
            for copy in to_x:
                copy.start()

        @pl.when(n == X_AT)
        def _():
            for copy in to_x:
                copy.wait()
            level = jnp.concatenate([xnodes[i] for i in range(NX)], axis=0)
            level = pair_up(up_tr, 4, rows(level, (0, 2)), rows(level, (1, 3)))
            for i in range(2):
                nodes5[i] = rows(level, (i,))
            roots[b] = pair_up(up_tr, 5, rows(level, (0,)), rows(level, (1,)))
            for copy in to_z:
                copy.start()

    for index in range(6, 15):
        loads[index].wait()

    @pl.loop(0, LEAVES // 8)
    def _(step):
        for inner in range(8):
            n = step * 8 + inner
            total = jnp.zeros((SCEN, RANK), f32)
            for slot in range(FAR):
                total = total + dot3(coef[window_index(far[slot, n])], coupling[n, slot])
            local[n] = total

    @pl.loop(0, LEAVES // 4)
    def _(step):
        for inner in range(4):
            n = step * 4 + inner
            row_halves = halves(rowb[n])
            out[n] = out[n] + split_dot(halves(local[n]), row_halves, 1, 0)
            down_high[n], down_low[n] = halves(split_dot(halves(leaf_down[n]), row_halves, 0, 0))

    siblings = (
        partner0[...],
        ynodes[flipped(y)],
        nodes2[flipped(y // 2)],
        nodes3[flipped(y // 4)],
        xnodes[flipped(x)],
        nodes5[flipped(x // 2)],
    )
    side = (core, y % 2, (y // 2) % 2, y // 4, x % 2, x // 2)
    known = jnp.zeros((SCEN, RANK), f32)
    for level in reversed(range(LEVELS)):
        known = dot3(siblings[level], sibling[level, side[level]]) + dot3(known, down_tr[level, side[level]])
    chain = down_tr[0, side[0]]
    for level in range(1, LEVELS):
        chain = dot3(chain, down_tr[level, side[level]], 0)
    chain_halves = halves(chain)
    for copy in to_z:
        copy.wait()
    top = jnp.zeros((SCEN, RANK), f32)
    for i in range(NZ - 1):
        top = top + dot3(roots[(b + 1 + i) % NZ], branch[i])
    halved = halves(known + split_dot(halves(top), chain_halves, 1, 1))

    @pl.loop(0, LEAVES // 8)
    def _(step):
        for inner in range(8):
            n = step * 8 + inner
            out[n] = out[n] + split_dot(halved, (down_high[n], down_low[n]), 1, 0)


def on_device(charges, coords, areas, col, row, up, down, coupling, up_tr, down_tr, sib, branch, near, far):
    window = 3 * LEAVES
    hbm = pl.BlockSpec(memory_space=pltpu.HBM)
    node = (SCEN, RANK)
    square = (RANK, RANK)
    leaf_shape = (LEAVES, SCEN, PANELS)
    down_shape = (LEAVES, RANK, PANELS)
    made = (
        ((window, FEATURES, PANELS), bf16),
        ((window, 2 * SCEN, PANELS), bf16),
        ((LEAVES, FEATURES, PANELS), bf16),
        ((window,) + node, f32),
        (node, f32),
        (node, f32),
    )

    def vmem(*shape):
        return pltpu.VMEM(shape, f32)

    def params(collective_id, limit):
        return pltpu.CompilerParams(
            collective_id=collective_id, has_side_effects=True, vmem_limit_bytes=limit
        )

    scratch = [pltpu.VMEM(shape, kind) for shape, kind in made]
    transfer = vmem(LEVELS, 2, *square)
    source, weight, target, coef, pair, partner = pl.pallas_call(
        exchange,
        out_shape=[jax.ShapeDtypeStruct(shape, kind) for shape, kind in made],
        in_specs=[hbm] * 6,
        out_specs=[hbm] * 6,
        scratch_shapes=[
            vmem(window, SCEN, PANELS),
            vmem(3, window, PANELS),
            vmem(window, PANELS),
            vmem(LEAVES, RANK, PANELS),
            vmem(LEAVES, *square),
            transfer,
            vmem(*node),
        ]
        + scratch
        + [
            pltpu.SemaphoreType.DMA((6,)),
            pltpu.SemaphoreType.DMA((10,)),
            pltpu.SemaphoreType.DMA((9,)),
            pltpu.SemaphoreType.DMA((9,)),
        ],
        compiler_params=params(0, FULL_VMEM),
        name="exchange",
    )(charges, jnp.transpose(coords, (1, 0, 2)), areas, col, up, up_tr[0])
    return pl.pallas_call(
        near_field,
        out_shape=jax.ShapeDtypeStruct(leaf_shape, f32),
        in_specs=[hbm] * 15,
        out_specs=pl.BlockSpec(memory_space=pltpu.VMEM),
        scratch_shapes=[
            pltpu.SMEM((LEAVES, NEAR), jnp.int32),
            pltpu.SMEM((FAR, LEAVES), jnp.int32),
            scratch[0],
            scratch[2],
            scratch[1],
            scratch[3],
            scratch[5],
            vmem(LEAVES, FAR, *square),
            vmem(LEAVES, *square),
            vmem(LEAVES, RANK, PANELS),
            transfer,
            transfer,
            transfer,
            vmem(NZ - 1, *square),
            vmem(LEAVES, *node),
            pltpu.VMEM(down_shape, bf16),
            pltpu.VMEM(down_shape, bf16),
            vmem(NY, *node),
            vmem(4, *node),
            vmem(2, *node),
            vmem(NX, *node),
            vmem(2, *node),
            vmem(NZ, *node),
            pltpu.SemaphoreType.DMA((15,)),
            pltpu.SemaphoreType.DMA((17,)),
            pltpu.SemaphoreType.DMA((17,)),
        ],
        compiler_params=params(1, FULL_VMEM),
        name="near_field",
    )(
        near,
        far.T,
        source,
        target,
        weight,
        coef,
        pair,
        partner,
        coupling,
        down,
        row,
        up_tr[0],
        sib[0],
        down_tr[0],
        branch[0],
    )


def solution(mesh):
    leaf = ("branch", "cluster")

    def spec(axis, rank):
        return P(axis, *([None] * (rank - 1)))

    in_specs = (
        spec(leaf, 3),
        spec(leaf, 3),
        spec(leaf, 2),
        spec(leaf, 3),
        spec(leaf, 3),
        spec(leaf, 3),
        spec(leaf, 3),
        spec(leaf, 4),
        spec("branch", 5),
        spec("branch", 5),
        spec("branch", 5),
        spec("branch", 4),
        spec(leaf, 2),
        spec(leaf, 2),
    )
    return jax.shard_map(
        on_device, mesh=mesh, in_specs=in_specs, out_specs=spec(leaf, 3), check_vma=False
    )
```

time: 58.9 us -> 52.9 us (0.90)
  the two profiles are of different devices: /device:TPU:8 before, /device:TPU:4 now
where the time goes in v3:
time: 52.9 us; the launch traced here: 52.7 us
  Pallas kernels  51 us (96%)
  local copies, waits for them, and re-layouts  1.67 us (3%)
    pallas_call x1, Pallas kernels, on_device(): pl.pallas_call(near_field, out_shape=jax.ShapeDtypeStruct(leaf_shape, f32...  39.2 us
    pallas_call x1, Pallas kernels, on_device(): pl.pallas_call(exchange, out_shape=[jax.ShapeDtypeStruct(shape, kind) for...  11.8 us
    unnamed x1, local copies, waits for them, and re-layouts  1.67 us

profile of v3, /device:TPU:4, one launch (start us, length us, event | category | flops | bytes accessed | tf_op | source)
XLA Modules:
  0.0 52.7 jit_solution(1223292523926251303)
XLA Ops:
  0.0 11.8 %exchange.1 = (bf16[48,32,256]{2,1,0:T(8,128)(2,1)}, bf16[48,32,256]{2,1,0:T(8,128)(2,1)}, bf16[16,32,256]{2,1,0:T(8,128)(2,1)}, f32[48,16,64]{2,1,0:T(8,128)}, f32[16,64]{1,0:T(8,128)}, /*index=5*/f32[16,64]{1,0:T(8,128)}) custom-call(f32[16,16,256]{2,1,0:T(8,128)} %charges_hbm.1, f32[3,16,256]{2,1,0:T(8,128)} %bitcast.11, f32[16,256]{1,0:T(8,128)} %areas_hbm.1, ...), custom_call_target="tpu_custom_call" | custom-call | tf_op jit(solution)/shard_map/exchange/pallas_call | solution.py:486
  11.8 39.2 %near_field.1 = f32[16,16,256]{2,1,0:T(8,128)} custom-call(s32[16,16]{1,0:T(8,128)} %near_hbm.1, s32[4,16]{1,0:T(4,128)} %bitcast.12, bf16[48,32,256]{2,1,0:T(8,128)(2,1)} %get-tuple-element.11.source_hbm, bf16[16,32,256]{2,1,0:T(8,128)(2,1)} %get-tuple-element.12.target_hbm, bf16[48,32,256]{2,1,0:T(8,128)(2,1)} %get-tuple-element.13.weight_hbm, ...), custom_call_target="tpu_custom_call" | custom-call | tf_op jit(solution)/shard_map/near_field/pallas_call | solution.py:510
  51.0 1.7 %copy.16 = f32[16,16,256]{2,1,0:T(8,128)} copy(f32[16,16,256]{2,1,0:T(8,128)} %near_field.1) | data formatting | bytes 524288

commit v4 on v3

--- a/solution.py
+++ b/solution.py
@@ -18,7 +18,8 @@
 NX, NY, NZ, CLUSTERS = 4, 8, 8, 64
 FEATURES = 32
 FULL_VMEM = 67043328
-BARRIER_AT, Y_AT, X_AT = 3, 6, 8
+GROUP = 2
+BARRIER_AT, Y_AT, X_AT = 1, 2, 3
 PAIRS = ((0, 0), (0, 1), (1, 0), (0, 2), (2, 0), (1, 1), (1, 2), (2, 1))
 
 
@@ -119,18 +120,31 @@
     col_hbm,
     up_hbm,
     up_tr_hbm,
+    down_hbm,
+    row_hbm,
+    down_tr_hbm,
+    sibling_hbm,
+    branch_hbm,
     source_out,
     weight_out,
     target_out,
     coef_out,
     pair_out,
     partner_out,
+    way_out,
+    high_out,
+    low_out,
     charges,
     coords,
     areas,
     col,
     leaf_up,
     up_tr,
+    leaf_down,
+    rowb,
+    down_tr,
+    sibling,
+    branch,
     node0,
     source,
     weight,
@@ -138,6 +152,9 @@
     coef,
     pair,
     partner0,
+    way,
+    down_high,
+    down_low,
     local_sem,
     out_sem,
     send_sem,
@@ -159,6 +176,11 @@
             (col_hbm, col),
             (up_hbm, leaf_up),
             (up_tr_hbm, up_tr),
+            (down_tr_hbm, down_tr),
+            (sibling_hbm, sibling),
+            (branch_hbm, branch),
+            (down_hbm, leaf_down),
+            (row_hbm, rowb),
         ),
         local_sem,
     )
@@ -173,8 +195,7 @@
     coords_copies = sides(coords, 0, True)
     areas_copies = sides(areas, 2, False)
     charges_copies = sides(charges, 4, False)
-    coef_copies = sides(coef, 6, False)
-    to_partner = send(node0, partner0, 8, partner)
+    to_partner = send(node0, partner0, 6, partner)
 
     for index in range(3):
         loads[index].wait()
@@ -188,16 +209,14 @@
     def _(step):
         for inner in range(8):
             n = step * 8 + inner
-            coef[LEAVES + n] = dot3(charges[LEAVES + n], col[n])
-
-    for copy in coef_copies:
-        copy.start()
+            coef[n] = dot3(charges[LEAVES + n], col[n])
+
     loads[4].wait()
 
     def add_leaf(step, total):
         for inner in range(8):
             n = step * 8 + inner
-            total = total + dot3(coef[LEAVES + n], leaf_up[n])
+            total = total + dot3(coef[n], leaf_up[n])
         return total
 
     node0[...] = lax.fori_loop(0, LEAVES // 8, add_leaf, jnp.zeros((SCEN, RANK), f32))
@@ -232,6 +251,7 @@
         copy.start()
         parts.append(copy)
 
+    store(coef, coef_out)
     store(target, target_out)
     store(source.at[own], source_out.at[own])
     store(weight.at[own], weight_out.at[own])
@@ -244,6 +264,29 @@
     store(pair, pair_out)
     store(partner0, partner_out)
 
+    for index in range(6, 11):
+        loads[index].wait()
+    side = (core, y % 2, (y // 2) % 2, y // 4, x % 2, x // 2)
+    way[0] = sibling[0, side[0]]
+    path = down_tr[0, side[0]]
+    for level in range(1, LEVELS):
+        way[level] = dot3(path, sibling[level, side[level]], 0)
+        path = dot3(path, down_tr[level, side[level]], 0)
+    path_halves = halves(path)
+    for i in range(NZ - 1):
+        way[LEVELS + i] = split_dot(path_halves, halves(branch[i]), 1, 0)
+    store(way, way_out)
+
+    @pl.loop(0, LEAVES // 8)
+    def _(step):
+        for inner in range(8):
+            n = step * 8 + inner
+            product = split_dot(halves(leaf_down[n]), halves(rowb[n]), 0, 0)
+            down_high[n], down_low[n] = halves(product)
+
+    store(down_high, high_out)
+    store(down_low, low_out)
+
     for copy in coords_copies:
         copy.wait()
 
@@ -268,9 +311,6 @@
 
     store(weight.at[low_side], weight_out.at[low_side])
     store(weight.at[high_side], weight_out.at[high_side])
-    for copy in coef_copies:
-        copy.wait()
-    store(coef, coef_out)
     for copy in parts:
         copy.wait()
 
@@ -285,12 +325,11 @@
     pair_hbm,
     partner_hbm,
     coupling_hbm,
-    down_hbm,
     row_hbm,
     up_tr_hbm,
-    sibling_hbm,
-    down_tr_hbm,
-    branch_hbm,
+    way_hbm,
+    high_hbm,
+    low_hbm,
     out,
     near,
     far,
@@ -300,12 +339,9 @@
     coef,
     partner0,
     coupling,
-    leaf_down,
     rowb,
     up_tr,
-    sibling,
-    down_tr,
-    branch,
+    way,
     local,
     down_high,
     down_low,
@@ -323,7 +359,10 @@
     y_peers = [(b, (x * NY + (y + k) % NY) * 2 + core) for k in range(1, NY)]
     x_peers = [(b, (((x + k) % NX) * NY + y) * 2 + core) for k in range(1, NX)]
     z_peers = [((b + k) % NZ, c) for k in range(1, NZ)]
-    wait_for_all = greet(y_peers + x_peers + z_peers)
+    left = (b, (c + CLUSTERS - 1) % CLUSTERS)
+    right = (b, (c + 1) % CLUSTERS)
+    own = pl.ds(LEAVES, LEAVES)
+    wait_for_all = greet([left, right] + y_peers + x_peers + z_peers)
     loads = start_loads(
         (
             (near_hbm, near),
@@ -332,15 +371,14 @@
             (weight_hbm, weight),
             (pair_hbm, ynodes.at[y]),
             (up_tr_hbm, up_tr),
+            (coef_hbm, coef.at[own]),
             (far_hbm, far),
-            (coef_hbm, coef),
             (coupling_hbm, coupling),
             (row_hbm, rowb),
-            (down_hbm, leaf_down),
             (partner_hbm, partner0),
-            (sibling_hbm, sibling),
-            (down_tr_hbm, down_tr),
-            (branch_hbm, branch),
+            (way_hbm, way),
+            (high_hbm, down_high),
+            (low_hbm, down_low),
         ),
         local_sem,
     )
@@ -351,6 +389,10 @@
     to_y = [send(ynodes.at[y], ynodes.at[y], k, peer) for k, peer in enumerate(y_peers)]
     to_x = [send(xnodes.at[x], xnodes.at[x], 7 + k, peer) for k, peer in enumerate(x_peers)]
     to_z = [send(roots.at[b], roots.at[b], 10 + k, peer) for k, peer in enumerate(z_peers)]
+    to_sides = [
+        send(coef.at[own], coef.at[pl.ds(2 * LEAVES, LEAVES)], 17, left),
+        send(coef.at[own], coef.at[pl.ds(0, LEAVES)], 18, right),
+    ]
     for index in range(4):
         loads[index].wait()
     shift = LEAVES - (b * CLUSTERS + c) * LEAVES
@@ -358,29 +400,35 @@
     def window_index(leaf):
         return jnp.minimum(jnp.maximum(leaf + shift, 0), 3 * LEAVES - 1)
 
-    @pl.loop(0, LEAVES)
-    def _(n):
-        tn = target[n]
-        high_sum = jnp.zeros((2 * SCEN, PANELS), f32)
-        low_sum = jnp.zeros((SCEN, PANELS), f32)
-        for slot in range(NEAR):
-            m = window_index(near[n, slot])
-            kernel = lax.rsqrt(dot(source[m], tn, 0, 0))
-            kernel_high, kernel_low = halves(kernel)
-            wm = weight[m]
-            high_sum = high_sum + dot(wm, kernel_high, 1, 0)
-            low_sum = low_sum + dot(wm[:SCEN], kernel_low, 1, 0)
-        out[n] = high_sum[:SCEN] + high_sum[SCEN:] + low_sum
-
-        @pl.when(n == BARRIER_AT)
+    @pl.loop(0, LEAVES // GROUP)
+    def _(step):
+        found = []
+        for inner in range(GROUP):
+            n = step * GROUP + inner
+            tn = target[n]
+            high_sum = jnp.zeros((2 * SCEN, PANELS), f32)
+            low_sum = jnp.zeros((SCEN, PANELS), f32)
+            for slot in range(NEAR):
+                m = window_index(near[n, slot])
+                kernel = lax.rsqrt(dot(source[m], tn, 0, 0))
+                kernel_high, kernel_low = halves(kernel)
+                wm = weight[m]
+                high_sum = high_sum + dot(wm, kernel_high, 1, 0)
+                low_sum = low_sum + dot(wm[:SCEN], kernel_low, 1, 0)
+            found.append((n, high_sum[:SCEN] + high_sum[SCEN:] + low_sum))
+        for n, value in found:
+            out[n] = value
+
+        @pl.when(step == BARRIER_AT)
         def _():
             loads[4].wait()
             loads[5].wait()
+            loads[6].wait()
             wait_for_all()
-            for copy in to_y:
+            for copy in to_y + to_sides:
                 copy.start()
 
-        @pl.when(n == Y_AT)
+        @pl.when(step == Y_AT)
         def _():
             for copy in to_y:
                 copy.wait()
@@ -395,7 +443,7 @@
             for copy in to_x:
                 copy.start()
 
-        @pl.when(n == X_AT)
+        @pl.when(step == X_AT)
         def _():
             for copy in to_x:
                 copy.wait()
@@ -407,25 +455,18 @@
             for copy in to_z:
                 copy.start()
 
-    for index in range(6, 15):
+    for index in range(7, 14):
         loads[index].wait()
-
-    @pl.loop(0, LEAVES // 8)
-    def _(step):
-        for inner in range(8):
-            n = step * 8 + inner
-            total = jnp.zeros((SCEN, RANK), f32)
-            for slot in range(FAR):
-                total = total + dot3(coef[window_index(far[slot, n])], coupling[n, slot])
-            local[n] = total
-
-    @pl.loop(0, LEAVES // 4)
-    def _(step):
-        for inner in range(4):
-            n = step * 4 + inner
-            row_halves = halves(rowb[n])
-            out[n] = out[n] + split_dot(halves(local[n]), row_halves, 1, 0)
-            down_high[n], down_low[n] = halves(split_dot(halves(leaf_down[n]), row_halves, 0, 0))
+    for copy in to_sides:
+        copy.wait()
+
+    for n in range(LEAVES):
+        total = jnp.zeros((SCEN, RANK), f32)
+        for slot in range(FAR):
+            total = total + dot3(coef[window_index(far[slot, n])], coupling[n, slot])
+        local[n] = total
+    for n in range(LEAVES):
+        out[n] = out[n] + split_dot(halves(local[n]), halves(rowb[n]), 1, 0)
 
     siblings = (
         partner0[...],
@@ -435,20 +476,14 @@
         xnodes[flipped(x)],
         nodes5[flipped(x // 2)],
     )
-    side = (core, y % 2, (y // 2) % 2, y // 4, x % 2, x // 2)
-    known = jnp.zeros((SCEN, RANK), f32)
-    for level in reversed(range(LEVELS)):
-        known = dot3(siblings[level], sibling[level, side[level]]) + dot3(known, down_tr[level, side[level]])
-    chain = down_tr[0, side[0]]
-    for level in range(1, LEVELS):
-        chain = dot3(chain, down_tr[level, side[level]], 0)
-    chain_halves = halves(chain)
+    down = jnp.zeros((SCEN, RANK), f32)
+    for level in range(LEVELS):
+        down = down + dot3(siblings[level], way[level])
     for copy in to_z:
         copy.wait()
-    top = jnp.zeros((SCEN, RANK), f32)
     for i in range(NZ - 1):
-        top = top + dot3(roots[(b + 1 + i) % NZ], branch[i])
-    halved = halves(known + split_dot(halves(top), chain_halves, 1, 1))
+        down = down + dot3(roots[(b + 1 + i) % NZ], way[LEVELS + i])
+    halved = halves(down)
 
     @pl.loop(0, LEAVES // 8)
     def _(step):
@@ -468,9 +503,12 @@
         ((window, FEATURES, PANELS), bf16),
         ((window, 2 * SCEN, PANELS), bf16),
         ((LEAVES, FEATURES, PANELS), bf16),
-        ((window,) + node, f32),
+        ((LEAVES,) + node, f32),
         (node, f32),
         (node, f32),
+        ((LEVELS + NZ - 1,) + square, f32),
+        (down_shape, bf16),
+        (down_shape, bf16),
     )
 
     def vmem(*shape):
@@ -483,11 +521,11 @@
 
     scratch = [pltpu.VMEM(shape, kind) for shape, kind in made]
     transfer = vmem(LEVELS, 2, *square)
-    source, weight, target, coef, pair, partner = pl.pallas_call(
+    source, weight, target, coef, pair, partner, way, high, low = pl.pallas_call(
         exchange,
         out_shape=[jax.ShapeDtypeStruct(shape, kind) for shape, kind in made],
-        in_specs=[hbm] * 6,
-        out_specs=[hbm] * 6,
+        in_specs=[hbm] * 11,
+        out_specs=[hbm] * 9,
         scratch_shapes=[
             vmem(window, SCEN, PANELS),
             vmem(3, window, PANELS),
@@ -495,22 +533,39 @@
             vmem(LEAVES, RANK, PANELS),
             vmem(LEAVES, *square),
             transfer,
+            vmem(LEAVES, *square),
+            vmem(LEAVES, RANK, PANELS),
+            transfer,
+            transfer,
+            vmem(NZ - 1, *square),
             vmem(*node),
         ]
         + scratch
         + [
-            pltpu.SemaphoreType.DMA((6,)),
-            pltpu.SemaphoreType.DMA((10,)),
-            pltpu.SemaphoreType.DMA((9,)),
-            pltpu.SemaphoreType.DMA((9,)),
+            pltpu.SemaphoreType.DMA((11,)),
+            pltpu.SemaphoreType.DMA((13,)),
+            pltpu.SemaphoreType.DMA((7,)),
+            pltpu.SemaphoreType.DMA((7,)),
         ],
         compiler_params=params(0, FULL_VMEM),
         name="exchange",
-    )(charges, jnp.transpose(coords, (1, 0, 2)), areas, col, up, up_tr[0])
+    )(
+        charges,
+        jnp.transpose(coords, (1, 0, 2)),
+        areas,
+        col,
+        up,
+        up_tr[0],
+        down,
+        row,
+        down_tr[0],
+        sib[0],
+        branch[0],
+    )
     return pl.pallas_call(
         near_field,
         out_shape=jax.ShapeDtypeStruct(leaf_shape, f32),
-        in_specs=[hbm] * 15,
+        in_specs=[hbm] * 14,
         out_specs=pl.BlockSpec(memory_space=pltpu.VMEM),
         scratch_shapes=[
             pltpu.SMEM((LEAVES, NEAR), jnp.int32),
@@ -518,15 +573,12 @@
             scratch[0],
             scratch[2],
             scratch[1],
-            scratch[3],
+            vmem(window, *node),
             scratch[5],
             vmem(LEAVES, FAR, *square),
-            vmem(LEAVES, *square),
             vmem(LEAVES, RANK, PANELS),
             transfer,
-            transfer,
-            transfer,
-            vmem(NZ - 1, *square),
+            scratch[6],
             vmem(LEAVES, *node),
             pltpu.VMEM(down_shape, bf16),
             pltpu.VMEM(down_shape, bf16),
@@ -536,9 +588,9 @@
             vmem(NX, *node),
             vmem(2, *node),
             vmem(NZ, *node),
-            pltpu.SemaphoreType.DMA((15,)),
-            pltpu.SemaphoreType.DMA((17,)),
-            pltpu.SemaphoreType.DMA((17,)),
+            pltpu.SemaphoreType.DMA((14,)),
+            pltpu.SemaphoreType.DMA((19,)),
+            pltpu.SemaphoreType.DMA((19,)),
         ],
         compiler_params=params(1, FULL_VMEM),
         name="near_field",
@@ -552,12 +604,11 @@
         pair,
         partner,
         coupling,
-        down,
         row,
         up_tr[0],
-        sib[0],
-        down_tr[0],
-        branch[0],
+        way,
+        high,
+        low,
     )
 
 

time: 52.9 us -> 48.3 us (0.913)
  the two profiles are of different devices: /device:TPU:4 before, /device:TPU:64 now
where the time goes in v4:
time: 48.3 us; the launch traced here: 48.1 us
  Pallas kernels  46.4 us (96%)
  local copies, waits for them, and re-layouts  1.67 us (3%)
    pallas_call x1, Pallas kernels, on_device(): pl.pallas_call(near_field, out_shape=jax.ShapeDtypeStruct(leaf_shape, f32...  33.5 us
    pallas_call x1, Pallas kernels, on_device(): pl.pallas_call(exchange, out_shape=[jax.ShapeDtypeStruct(shape, kind) for...  12.9 us
    unnamed x1, local copies, waits for them, and re-layouts  1.67 us

profile of v4, /device:TPU:64, one launch (start us, length us, event | category | flops | bytes accessed | tf_op | source)
XLA Modules:
  0.0 48.1 jit_solution(17875565923753390347)
XLA Ops:
  0.0 12.9 %exchange.1 = (bf16[48,32,256]{2,1,0:T(8,128)(2,1)}, bf16[48,32,256]{2,1,0:T(8,128)(2,1)}, bf16[16,32,256]{2,1,0:T(8,128)(2,1)}, f32[16,16,64]{2,1,0:T(8,128)}, ...) custom-call(f32[16,16,256]{2,1,0:T(8,128)} %charges_hbm.1, ...), custom_call_target="tpu_custom_call" | custom-call | tf_op jit(solution)/shard_map/exchange/pallas_call | solution.py:524
  12.9 33.5 %near_field.1 = f32[16,16,256]{2,1,0:T(8,128)} custom-call(s32[16,16]{1,0:T(8,128)} %near_hbm.1, s32[4,16]{1,0:T(4,128)} %bitcast.12, bf16[48,32,256]{2,1,0:T(8,128)(2,1)} %get-tuple-element.14.source_hbm, bf16[16,32,256]{2,1,0:T(8,128)(2,1)} %get-tuple-element.15.target_hbm, bf16[48,32,256]{2,1,0:T(8,128)(2,1)} %get-tuple-element.16.weight_hbm, ...), custom_call_target="tpu_custom_call" | custom-call | tf_op jit(solution)/shard_map/near_field/pallas_call | solution.py:565
  46.4 1.7 %copy.16 = f32[16,16,256]{2,1,0:T(8,128)} copy(f32[16,16,256]{2,1,0:T(8,128)} %near_field.1) | data formatting | bytes 524288

commit v5 on v4

--- a/solution.py
+++ b/solution.py
@@ -17,9 +17,9 @@
 NEAR, FAR, LEVELS = 16, 4, 6
 NX, NY, NZ, CLUSTERS = 4, 8, 8, 64
 FEATURES = 32
-FULL_VMEM = 67043328
+KERNEL_VMEM = 67043328 - (6 << 20)
 GROUP = 2
-BARRIER_AT, Y_AT, X_AT = 1, 2, 3
+BARRIER_AT, Y_AT, X_AT = 2, 3, 4
 PAIRS = ((0, 0), (0, 1), (1, 0), (0, 2), (2, 0), (1, 1), (1, 2), (2, 1))
 
 
@@ -125,15 +125,15 @@
     down_tr_hbm,
     sibling_hbm,
     branch_hbm,
-    source_out,
-    weight_out,
-    target_out,
-    coef_out,
-    pair_out,
+    source,
+    weight,
+    target,
+    coef,
+    pair,
     partner_out,
-    way_out,
-    high_out,
-    low_out,
+    way,
+    down_high,
+    down_low,
     charges,
     coords,
     areas,
@@ -146,17 +146,8 @@
     sibling,
     branch,
     node0,
-    source,
-    weight,
-    target,
-    coef,
-    pair,
     partner0,
-    way,
-    down_high,
-    down_low,
     local_sem,
-    out_sem,
     send_sem,
     recv_sem,
 ):
@@ -244,25 +235,12 @@
             target[n] = features_of(LEAVES + n, False)
             weigh(LEAVES + n)
 
-    parts = []
-
-    def store(ref, hbm):
-        copy = pltpu.make_async_copy(ref, hbm, out_sem.at[len(parts)])
-        copy.start()
-        parts.append(copy)
-
-    store(coef, coef_out)
-    store(target, target_out)
-    store(source.at[own], source_out.at[own])
-    store(weight.at[own], weight_out.at[own])
-
     loads[5].wait()
     to_partner.wait()
     mine, other = node0[...], partner0[...]
     even = core == 0
     pair[...] = pair_up(up_tr, 0, jnp.where(even, mine, other), jnp.where(even, other, mine))
-    store(pair, pair_out)
-    store(partner0, partner_out)
+    partner_out[...] = other
 
     for index in range(6, 11):
         loads[index].wait()
@@ -275,7 +253,6 @@
     path_halves = halves(path)
     for i in range(NZ - 1):
         way[LEVELS + i] = split_dot(path_halves, halves(branch[i]), 1, 0)
-    store(way, way_out)
 
     @pl.loop(0, LEAVES // 8)
     def _(step):
@@ -284,8 +261,6 @@
             product = split_dot(halves(leaf_down[n]), halves(rowb[n]), 0, 0)
             down_high[n], down_low[n] = halves(product)
 
-    store(down_high, high_out)
-    store(down_low, low_out)
 
     for copy in coords_copies:
         copy.wait()
@@ -297,8 +272,6 @@
             source[n] = features_of(n, True)
             source[2 * LEAVES + n] = features_of(2 * LEAVES + n, True)
 
-    store(source.at[low_side], source_out.at[low_side])
-    store(source.at[high_side], source_out.at[high_side])
     for copy in areas_copies + charges_copies:
         copy.wait()
 
@@ -309,42 +282,30 @@
             weigh(n)
             weigh(2 * LEAVES + n)
 
-    store(weight.at[low_side], weight_out.at[low_side])
-    store(weight.at[high_side], weight_out.at[high_side])
-    for copy in parts:
-        copy.wait()
-
 
 def near_field(
     near_hbm,
     far_hbm,
-    source_hbm,
-    target_hbm,
-    weight_hbm,
-    coef_hbm,
-    pair_hbm,
-    partner_hbm,
+    source,
+    target,
+    weight,
+    own_coef,
+    pair,
+    partner0,
     coupling_hbm,
     row_hbm,
     up_tr_hbm,
-    way_hbm,
-    high_hbm,
-    low_hbm,
+    way,
+    down_high,
+    down_low,
     out,
     near,
     far,
-    source,
-    target,
-    weight,
     coef,
-    partner0,
     coupling,
     rowb,
     up_tr,
-    way,
     local,
-    down_high,
-    down_low,
     ynodes,
     nodes2,
     nodes3,
@@ -366,19 +327,10 @@
     loads = start_loads(
         (
             (near_hbm, near),
-            (target_hbm, target),
-            (source_hbm, source),
-            (weight_hbm, weight),
-            (pair_hbm, ynodes.at[y]),
             (up_tr_hbm, up_tr),
-            (coef_hbm, coef.at[own]),
             (far_hbm, far),
             (coupling_hbm, coupling),
             (row_hbm, rowb),
-            (partner_hbm, partner0),
-            (way_hbm, way),
-            (high_hbm, down_high),
-            (low_hbm, down_low),
         ),
         local_sem,
     )
@@ -393,8 +345,9 @@
         send(coef.at[own], coef.at[pl.ds(2 * LEAVES, LEAVES)], 17, left),
         send(coef.at[own], coef.at[pl.ds(0, LEAVES)], 18, right),
     ]
-    for index in range(4):
-        loads[index].wait()
+    ynodes[y] = pair[...]
+    coef[own] = own_coef[...]
+    loads[0].wait()
     shift = LEAVES - (b * CLUSTERS + c) * LEAVES
 
     def window_index(leaf):
@@ -421,9 +374,7 @@
 
         @pl.when(step == BARRIER_AT)
         def _():
-            loads[4].wait()
-            loads[5].wait()
-            loads[6].wait()
+            loads[1].wait()
             wait_for_all()
             for copy in to_y + to_sides:
                 copy.start()
@@ -455,7 +406,7 @@
             for copy in to_z:
                 copy.start()
 
-    for index in range(7, 14):
+    for index in range(2, 5):
         loads[index].wait()
     for copy in to_sides:
         copy.wait()
@@ -519,13 +470,14 @@
             collective_id=collective_id, has_side_effects=True, vmem_limit_bytes=limit
         )
 
-    scratch = [pltpu.VMEM(shape, kind) for shape, kind in made]
+    passed = [pltpu.VMEM(shape, kind) for shape, kind in made]
+    on_chip = pl.BlockSpec(memory_space=pltpu.VMEM)
     transfer = vmem(LEVELS, 2, *square)
     source, weight, target, coef, pair, partner, way, high, low = pl.pallas_call(
         exchange,
-        out_shape=[jax.ShapeDtypeStruct(shape, kind) for shape, kind in made],
+        out_shape=passed,
         in_specs=[hbm] * 11,
-        out_specs=[hbm] * 9,
+        out_specs=[on_chip] * 9,
         scratch_shapes=[
             vmem(window, SCEN, PANELS),
             vmem(3, window, PANELS),
@@ -539,15 +491,12 @@
             transfer,
             vmem(NZ - 1, *square),
             vmem(*node),
-        ]
-        + scratch
-        + [
+            vmem(*node),
             pltpu.SemaphoreType.DMA((11,)),
-            pltpu.SemaphoreType.DMA((13,)),
             pltpu.SemaphoreType.DMA((7,)),
             pltpu.SemaphoreType.DMA((7,)),
         ],
-        compiler_params=params(0, FULL_VMEM),
+        compiler_params=params(0, KERNEL_VMEM),
         name="exchange",
     )(
         charges,
@@ -562,37 +511,34 @@
         sib[0],
         branch[0],
     )
+    source, weight, target, coef, pair, partner, way, high, low = (
+        pltpu.with_memory_space_constraint(array, pltpu.VMEM)
+        for array in (source, weight, target, coef, pair, partner, way, high, low)
+    )
     return pl.pallas_call(
         near_field,
-        out_shape=jax.ShapeDtypeStruct(leaf_shape, f32),
-        in_specs=[hbm] * 14,
-        out_specs=pl.BlockSpec(memory_space=pltpu.VMEM),
+        out_shape=pltpu.VMEM(leaf_shape, f32),
+        in_specs=[hbm] * 2 + [on_chip] * 6 + [hbm] * 3 + [on_chip] * 3,
+        out_specs=on_chip,
         scratch_shapes=[
             pltpu.SMEM((LEAVES, NEAR), jnp.int32),
             pltpu.SMEM((FAR, LEAVES), jnp.int32),
-            scratch[0],
-            scratch[2],
-            scratch[1],
             vmem(window, *node),
-            scratch[5],
             vmem(LEAVES, FAR, *square),
             vmem(LEAVES, RANK, PANELS),
             transfer,
-            scratch[6],
             vmem(LEAVES, *node),
-            pltpu.VMEM(down_shape, bf16),
-            pltpu.VMEM(down_shape, bf16),
             vmem(NY, *node),
             vmem(4, *node),
             vmem(2, *node),
             vmem(NX, *node),
             vmem(2, *node),
             vmem(NZ, *node),
-            pltpu.SemaphoreType.DMA((14,)),
+            pltpu.SemaphoreType.DMA((5,)),
             pltpu.SemaphoreType.DMA((19,)),
             pltpu.SemaphoreType.DMA((19,)),
         ],
-        compiler_params=params(1, FULL_VMEM),
+        compiler_params=params(1, KERNEL_VMEM),
         name="near_field",
     )(
         near,

time: 48.3 us -> 44.4 us (0.919)
  Pallas kernels: 46.4 us -> 43.5 us
  local copies, waits for them, and re-layouts: 1.67 us -> 0.71 us
    pallas_call x2, Pallas kernels: 46.4 us -> 43.5 us  [the longest x1 31.6 us: on_device(): pl.pallas_call(near_field, out_shape=pltpu.VMEM(leaf_shape, f32), in_spec...]
    unnamed x1, local copies, waits for them, and re-layouts: 1.67 us -> 0.71 us
where the time goes in v5:
time: 44.4 us; the launch traced here: 44.2 us
  Pallas kernels  43.5 us (98%)
  local copies, waits for them, and re-layouts  0.71 us (2%)
    pallas_call x1, Pallas kernels, on_device(): pl.pallas_call(near_field, out_shape=pltpu.VMEM(leaf_shape, f32), in_spec...  31.6 us
    pallas_call x1, Pallas kernels, on_device(): pl.pallas_call(exchange, out_shape=passed, in_specs=[hbm] * 11, out_specs...  11.9 us

profile of v5, /device:TPU:64, one launch (start us, length us, event | category | flops | bytes accessed | tf_op | source)
XLA Modules:
  0.0 44.2 jit_solution(6663216039565715514)
XLA Ops:
  0.0 11.9 %exchange.1 = (bf16[48,32,256]{2,1,0:T(8,128)(2,1)S(1)}, bf16[48,32,256]{2,1,0:T(8,128)(2,1)S(1)}, bf16[16,32,256]{2,1,0:T(8,128)(2,1)S(1)}, f32[16,16,64]{2,1,0...) custom-call(f32[16,16,256]{2,1,0:T(8,128)} %charges_hbm.1, ...), custom_call_target="tpu_custom_call" | custom-call | tf_op jit(solution)/shard_map/exchange/pallas_call | solution.py:476
  11.9 31.6 %near_field.1 = f32[16,16,256]{2,1,0:T(8,128)S(1)} custom-call(s32[16,16]{1,0:T(8,128)} %near_hbm.1, s32[4,16]{1,0:T(4,128)} %bitcast.12, bf16[48,32,256]{2,1,0:T(8,128)(2,1)S(1)} %get-tuple-element.14.source, bf16[16,32,256]{2,1,0:T(8,128)(2,1)S(1)} %get-tuple-element.15.target, bf16[48,32,256]{2,1,0:T(8,128)(2,1)S(1)} %get-tuple-element.16.weight, ...), custom_call_target="tpu_custom_call" | custom-call | tf_op jit(solution)/shard_map/near_field/pallas_call | solution.py:518
  43.5 0.7 %copy.16 = f32[16,16,256]{2,1,0:T(8,128)} copy(f32[16,16,256]{2,1,0:T(8,128)S(1)} %near_field.1) | data formatting | bytes 524288

commit v6 on v5

--- a/solution.py
+++ b/solution.py
@@ -19,7 +19,7 @@
 FEATURES = 32
 KERNEL_VMEM = 67043328 - (6 << 20)
 GROUP = 2
-BARRIER_AT, Y_AT, X_AT = 2, 3, 4
+BARRIER_AT, Y_AT, X_AT = 2, 4, 5
 PAIRS = ((0, 0), (0, 1), (1, 0), (0, 2), (2, 0), (1, 1), (1, 2), (2, 1))
 
 

time: 44.4 us -> 44.4 us (level)
  no operation moved by 1% of the time
where the time goes in v6:
time: 44.4 us; the launch traced here: 44.2 us
  Pallas kernels  43.5 us (98%)
  local copies, waits for them, and re-layouts  0.71 us (2%)
    pallas_call x1, Pallas kernels, on_device(): pl.pallas_call(near_field, out_shape=pltpu.VMEM(leaf_shape, f32), in_spec...  31.6 us
    pallas_call x1, Pallas kernels, on_device(): pl.pallas_call(exchange, out_shape=passed, in_specs=[hbm] * 11, out_specs...  11.9 us

profile of v6, /device:TPU:64, one launch (start us, length us, event | category | flops | bytes accessed | tf_op | source)
XLA Modules:
  0.0 44.2 jit_solution(1426503826422559386)
XLA Ops:
  0.0 11.9 %exchange.1 = (bf16[48,32,256]{2,1,0:T(8,128)(2,1)S(1)}, bf16[48,32,256]{2,1,0:T(8,128)(2,1)S(1)}, bf16[16,32,256]{2,1,0:T(8,128)(2,1)S(1)}, f32[16,16,64]{2,1,0...) custom-call(f32[16,16,256]{2,1,0:T(8,128)} %charges_hbm.1, ...), custom_call_target="tpu_custom_call" | custom-call | tf_op jit(solution)/shard_map/exchange/pallas_call | solution.py:476
  11.9 31.6 %near_field.1 = f32[16,16,256]{2,1,0:T(8,128)S(1)} custom-call(s32[16,16]{1,0:T(8,128)} %near_hbm.1, s32[4,16]{1,0:T(4,128)} %bitcast.12, bf16[48,32,256]{2,1,0:T(8,128)(2,1)S(1)} %get-tuple-element.14.source, bf16[16,32,256]{2,1,0:T(8,128)(2,1)S(1)} %get-tuple-element.15.target, bf16[48,32,256]{2,1,0:T(8,128)(2,1)S(1)} %get-tuple-element.16.weight, ...), custom_call_target="tpu_custom_call" | custom-call | tf_op jit(solution)/shard_map/near_field/pallas_call | solution.py:518
  43.5 0.7 %copy.16 = f32[16,16,256]{2,1,0:T(8,128)} copy(f32[16,16,256]{2,1,0:T(8,128)S(1)} %near_field.1) | data formatting | bytes 524288

commit v7 on v6

--- a/solution.py
+++ b/solution.py
@@ -19,7 +19,7 @@
 FEATURES = 32
 KERNEL_VMEM = 67043328 - (6 << 20)
 GROUP = 2
-BARRIER_AT, Y_AT, X_AT = 2, 4, 5
+BARRIER_AT, Y_AT, X_AT = 1, 3, 4
 PAIRS = ((0, 0), (0, 1), (1, 0), (0, 2), (2, 0), (1, 1), (1, 2), (2, 1))
 
 

time: 44.4 us -> 43 us (0.968)
  Pallas kernels: 43.5 us -> 42.1 us
    pallas_call x1, Pallas kernels: 31.6 us -> 30.2 us  [on_device(): pl.pallas_call(near_field, out_shape=pltpu.VMEM(leaf_shape, f32), in_spec...]
where the time goes in v7:
time: 43 us; the launch traced here: 42.8 us
  Pallas kernels  42.1 us (98%)
  local copies, waits for them, and re-layouts  0.71 us (2%)
    pallas_call x1, Pallas kernels, on_device(): pl.pallas_call(near_field, out_shape=pltpu.VMEM(leaf_shape, f32), in_spec...  30.2 us
    pallas_call x1, Pallas kernels, on_device(): pl.pallas_call(exchange, out_shape=passed, in_specs=[hbm] * 11, out_specs...  11.9 us

profile of v7, /device:TPU:64, one launch (start us, length us, event | category | flops | bytes accessed | tf_op | source)
XLA Modules:
  0.0 42.8 jit_solution(6258753096828560848)
XLA Ops:
  0.0 11.9 %exchange.1 = (bf16[48,32,256]{2,1,0:T(8,128)(2,1)S(1)}, bf16[48,32,256]{2,1,0:T(8,128)(2,1)S(1)}, bf16[16,32,256]{2,1,0:T(8,128)(2,1)S(1)}, f32[16,16,64]{2,1,0...) custom-call(f32[16,16,256]{2,1,0:T(8,128)} %charges_hbm.1, ...), custom_call_target="tpu_custom_call" | custom-call | tf_op jit(solution)/shard_map/exchange/pallas_call | solution.py:476
  11.9 30.2 %near_field.1 = f32[16,16,256]{2,1,0:T(8,128)S(1)} custom-call(s32[16,16]{1,0:T(8,128)} %near_hbm.1, s32[4,16]{1,0:T(4,128)} %bitcast.12, bf16[48,32,256]{2,1,0:T(8,128)(2,1)S(1)} %get-tuple-element.14.source, bf16[16,32,256]{2,1,0:T(8,128)(2,1)S(1)} %get-tuple-element.15.target, bf16[48,32,256]{2,1,0:T(8,128)(2,1)S(1)} %get-tuple-element.16.weight, ...), custom_call_target="tpu_custom_call" | custom-call | tf_op jit(solution)/shard_map/near_field/pallas_call | solution.py:518
  42.1 0.7 %copy.16 = f32[16,16,256]{2,1,0:T(8,128)} copy(f32[16,16,256]{2,1,0:T(8,128)S(1)} %near_field.1) | data formatting | bytes 524288
